TPU v7x, 128 devices: a whole 4x4x4 slice. The times are simulated.
128 devices in a mesh: mu: 16 (over y, z_hi, core), nu: 8 (over z_lo, x).
Axes of the slice: x: 4, y: 4, z: 4 (z_hi: 2, z_lo: 2; z = z_hi * 2 + z_lo), core: 2. Of those that a mesh axis runs over, the one named last changes fastest.
Arguments:
- earlier_vectors: float32 [1024, 1024, 512], P('mu', 'nu'), may hold values from -0.72 to 0.72
- pivot_integral_columns: float32 [1024, 1024, 256], P('mu', 'nu'), may hold values from -6 to 6
- diagonal: float32 [1024, 1024], P('mu', 'nu'), may hold values from 2 to 60
- orbitals: float32 [1024, 40], replicated, may hold values from -0.1875 to 0.1875
- pivots: int32 [256], replicated, may hold values from 0 to 1048575, as said below
Outputs:
- transformed: float32 [256, 820], P(('mu', 'nu'))
- updated_diagonal: float32 [1024, 1024], P('mu', 'nu')
Inputs may be any that keep to these rules, and one draw needn't show every extreme that they name: The pivots are distinct. The pairs held by one device (a block of 64 first by 128 second AO indices) contain at most 8 pivots, and some block contains exactly 8.
All inputs are finite; a program needn't handle non-finite values.
Results may differ from a plain program's by a relative error of at most 0.0001.
Values sent between devices are 32-bit elements; how exact they have to be, the bound alone decides.
No kernel may reach another device: no remote copies, remote signals or barrier semaphores. Data moves between devices by JAX's collectives and lax.ppermute only.
A program may use at most 128 MiB of HBM per device.

v0:
```python
import functools

import jax
import jax.numpy as jnp
from jax import lax
from jax.experimental import pallas as pl
from jax.experimental.pallas import tpu as pltpu
from jax.sharding import Mesh, PartitionSpec as P

SLOTS = 8
LANES = 128
PEERS = ("y", "zh", "zl", "x")
f32, bf16 = jnp.float32, jnp.bfloat16
smem = pl.BlockSpec(memory_space=pltpu.SMEM)
vmem = pl.BlockSpec(memory_space=pltpu.VMEM)
hbm = pl.BlockSpec(memory_space=pl.ANY)


def exchange(value, axes):
    return lax.all_to_all(value, axes, split_axis=0, concat_axis=0, tiled=True)


def sibling(value):
    return lax.ppermute(value, "c", [(0, 1), (1, 0)])


def iota(shape, dim):
    return lax.broadcasted_iota(jnp.int32, shape, dim)


def split(value):
    upper = value.astype(bf16)
    return upper, (value - upper.astype(f32)).astype(bf16)


def dot(a, b):
    return jnp.dot(a, b, preferred_element_type=f32)


def dot_nt(a, b):
    return lax.dot_general(a, b, (((1,), (1,)), ((), ())), preferred_element_type=f32)


def params(mib):
    return pltpu.CompilerParams(vmem_limit_bytes=mib << 20)


def pick_kernel(me, pivots, diagonal, vectors, out, rows, spots, index, sems):
    count = pivots.shape[0]
    cols, depth = vectors.shape[1:]
    for slot in range(2 * SLOTS):
        index[slot] = 0

    def scan(j, found):
        pair = pivots[j]
        index[found] = ((pair >> 10) & 63) * cols + (pair & 127)
        owner = (pair >> 16) * 8 + ((pair & 1023) >> 7)
        return found + (owner == me[0]).astype(jnp.int32)

    found = lax.fori_loop(0, count, scan, 0, unroll=8)
    copies = []
    for slot in range(SLOTS):
        spot = index[slot]
        copies.append(
            pltpu.make_async_copy(
                vectors.at[spot >> 7, pl.ds(spot & 127, 1), :],
                rows.at[pl.ds(slot, 1), :],
                sems.at[slot],
            )
        )
        copies[-1].start()
    lane = iota((1, LANES), 1)
    for slot in range(SLOTS):
        spot = index[slot]
        line = diagonal[pl.ds(spot >> 7, 1), :]
        spots[pl.ds(slot, 1), :] = jnp.where(lane == (spot & 127), line, 0.0)
    for copy in copies:
        copy.wait()
    used = iota((SLOTS, 1), 0) < found
    picked = jnp.where(used, rows[...], 0.0)
    residual = jnp.sum(spots[...], axis=1, keepdims=True) - jnp.sum(picked * picked, axis=1, keepdims=True)
    scale = lax.rsqrt(jnp.maximum(jnp.where(used, residual, 1.0), 1.0))
    out[:, :, :depth] = jnp.broadcast_to(picked[None], (64, SLOTS, depth))
    out[:, :, depth:] = jnp.broadcast_to(scale[None], (64, SLOTS, LANES))


def pick(me, pivots, diagonal, vectors):
    depth = vectors.shape[2]
    return pl.pallas_call(
        pick_kernel,
        out_shape=jax.ShapeDtypeStruct((64, SLOTS, depth + LANES), f32),
        in_specs=[smem, smem, vmem, hbm],
        out_specs=vmem,
        scratch_shapes=[
            pltpu.VMEM((SLOTS, depth), f32),
            pltpu.VMEM((SLOTS, LANES), f32),
            pltpu.SMEM((2 * SLOTS,), jnp.int32),
            pltpu.SemaphoreType.DMA((SLOTS,)),
        ],
        name="pick",
    )(me, pivots, diagonal, vectors)


def transform_kernel(flip, me, orbitals, value, out, wide_hi, wide_lo, right2, half, square, *flat):
    step = pl.program_id(0)
    tall, cols, width = value.shape
    rows = half.shape[0]
    active = orbitals.shape[1]

    @pl.when(step == 0)
    def _():
        left = orbitals[pl.ds(pl.multiple_of((me[0] >> 3) * rows, rows), rows), :]
        right = orbitals[pl.ds(pl.multiple_of((me[0] & 7) * cols, cols), cols), :]
        high = (active * 8, active)
        spread_rows = jnp.where(iota(high, 0) // 8 == iota(high, 1), 1.0, 0.0).astype(bf16)
        long = (rows, rows * 8)
        spread_cols = jnp.where(iota(long, 0) == iota(long, 1) // 8, 1.0, 0.0).astype(bf16)
        full = (active * 8, rows * 8)
        same = iota(full, 0) % 8 == iota(full, 1) % 8
        for part, wide in zip(split(left), (wide_hi, wide_lo)):
            repeated = dot(dot_nt(spread_rows, part).astype(bf16), spread_cols)
            wide[...] = jnp.where(same, repeated, 0.0).astype(bf16)
        eye = jnp.where(iota((48, active), 0) == iota((48, active), 1), 1.0, 0.0).astype(bf16)
        upper, lower = [dot_nt(eye, part).astype(bf16) for part in split(right)]
        right2[:48, :cols] = upper
        right2[:48, cols:] = upper
        right2[48:, :cols] = lower
        right2[48:, cols:] = jnp.zeros_like(lower)

    for i in range(tall):
        both = dot(right2[...], jnp.concatenate(split(value[i]), axis=0))
        half[step * tall + i] = both[:active] + both[48 : 48 + active]

    target = flat[0] if flip else out

    @pl.when(step == pl.num_programs(0) - 1)
    def _():
        for q in range(0, active, 8):
            upper, lower = split(half[:, q : q + 8, :].reshape(rows * 8, width))
            hi, lo = wide_hi[8 * q :, :], wide_lo[8 * q :, :]
            part = dot(hi, upper) + dot(lo, upper) + dot(hi, lower)
            square[q:, q : q + 8, :] = part.reshape(active - q, 8, width)
        for p in range(active):
            target[p * (p + 1) // 2 : (p + 1) * (p + 2) // 2, :] = square[p, : p + 1, :]
        if flip:
            turned = target[...].T[:, : out.shape[2]]
            for i in range(8):
                for c in range(2):
                    out[c, 16 * i : 16 * i + 16, :] = turned[32 * i + 16 * c : 32 * i + 16 * c + 16, :]


def transform(me, orbitals, value, flip):
    rows, cols, width = value.shape
    active = orbitals.shape[1]
    pairs = active * (active + 1) // 2
    tall = 8
    shape = (2, width // 2, pairs) if flip else (pairs, width)
    scratch = [
        pltpu.VMEM((active * 8, rows * 8), bf16),
        pltpu.VMEM((active * 8, rows * 8), bf16),
        pltpu.VMEM((96, 2 * cols), bf16),
        pltpu.VMEM((rows, active, width), f32),
        pltpu.VMEM((active, active, width), f32),
    ]
    if flip:
        scratch.append(pltpu.VMEM((pl.cdiv(pairs, LANES) * LANES, width), f32))
    return pl.pallas_call(
        functools.partial(transform_kernel, flip),
        out_shape=jax.ShapeDtypeStruct(shape, f32),
        grid=(rows // tall,),
        in_specs=[
            smem,
            pl.BlockSpec(orbitals.shape, lambda i: (0, 0)),
            pl.BlockSpec((tall, cols, width), lambda i: (i, 0, 0)),
        ],
        out_specs=pl.BlockSpec(shape, lambda i: (0,) * len(shape)),
        scratch_shapes=scratch,
        compiler_params=params(52),
        cost_estimate=pl.CostEstimate(
            flops=6 * active * 8 * rows * 8 * width * 16, bytes_accessed=value.size * 4, transcendentals=0
        ),
        name="turn_columns" if flip else "turn_vectors",
    )(me, orbitals, value)


def choose_kernel(me, near_hot, far_hot, near, far, upper_v, lower_v, mine_c, got_c, part, rows_hi, rows_lo, scaling, keep_hi, keep_lo):
    slots, width = near.shape
    depth = width - LANES
    core = (me[0] >> 3) & 1
    near_hi, near_lo = split(near[...])
    far_hi, far_lo = split(far[...])
    hi = dot(near_hot[...], near_hi) + dot(far_hot[...], far_hi)
    lo = dot(near_hot[...], near_lo) + dot(far_hot[...], far_lo)
    hi16, lo16 = hi.astype(bf16), lo.astype(bf16)
    rows_hi[...] = hi16[:, :depth]
    rows_lo[...] = lo16[:, :depth]
    scale = hi[:, depth:] + lo[:, depth:]
    scaling[...] = scale.T[:8]
    keep_hi[...] = hi16.reshape(keep_hi.shape)
    keep_lo[...] = lo16.reshape(keep_lo.shape)
    home_hi = keep_hi[:, core].reshape(-1, width)
    home_lo = keep_lo[:, core].reshape(-1, width)
    moved = (
        dot_nt(home_hi[:, :depth], upper_v[...])
        + dot_nt(home_lo[:, :depth], upper_v[...])
        + dot_nt(home_hi[:, :depth], lower_v[...])
    )
    scale = home_hi[:, depth : depth + 1].astype(f32) + home_lo[:, depth : depth + 1].astype(f32)
    part[...] = (mine_c[core] + got_c[...] - moved) * scale


def choose(me, near_hot, far_hot, near, far, upper_v, lower_v, mine_c, got_c):
    count, slots = near_hot.shape
    width = near.shape[1]
    depth = width - LANES
    pairs = upper_v.shape[0]
    return pl.pallas_call(
        choose_kernel,
        out_shape=(
            jax.ShapeDtypeStruct((count // 2, pairs), f32),
            jax.ShapeDtypeStruct((count, depth), bf16),
            jax.ShapeDtypeStruct((count, depth), bf16),
            jax.ShapeDtypeStruct((8, count), f32),
        ),
        in_specs=[smem] + [vmem] * 8,
        out_specs=(vmem,) * 4,
        scratch_shapes=[pltpu.VMEM((8, 2, 16, width), bf16), pltpu.VMEM((8, 2, 16, width), bf16)],
        compiler_params=params(24),
        cost_estimate=pl.CostEstimate(flops=2 * 10**9, bytes_accessed=6 * 10**6, transcendentals=0),
        name="choose",
    )(me, near_hot, far_hot, near, far, upper_v, lower_v, mine_c, got_c)


def update_kernel(vectors, columns, diagonal, rows_hi, rows_lo, scaling, out):
    tall, cols, depth = vectors.shape
    count = columns.shape[2]
    upper, lower = split(vectors[...].reshape(tall * cols, depth))
    update = dot_nt(upper, rows_hi[...]) + dot_nt(lower, rows_hi[...]) + dot_nt(upper, rows_lo[...])
    fresh = (columns[...].reshape(tall * cols, count) - update) * scaling[:1, :]
    square = fresh * fresh
    folded = (square[:, :LANES] + square[:, LANES:]).reshape(tall, cols, LANES)
    out[...] = diagonal[...] - jnp.sum(jnp.swapaxes(folded, 1, 2), axis=1)


def update(vectors, columns, diagonal, rows_hi, rows_lo, scaling):
    rows, cols, depth = vectors.shape
    count = columns.shape[2]
    tall = 8
    return pl.pallas_call(
        update_kernel,
        out_shape=jax.ShapeDtypeStruct((rows, cols), f32),
        grid=(rows // tall,),
        in_specs=[
            pl.BlockSpec((tall, cols, depth), lambda i: (i, 0, 0)),
            pl.BlockSpec((tall, cols, count), lambda i: (i, 0, 0)),
            pl.BlockSpec((tall, cols), lambda i: (i, 0)),
            pl.BlockSpec((count, depth), lambda i: (0, 0)),
            pl.BlockSpec((count, depth), lambda i: (0, 0)),
            pl.BlockSpec((8, count), lambda i: (0, 0)),
        ],
        out_specs=pl.BlockSpec((tall, cols), lambda i: (i, 0)),
        compiler_params=params(52),
        cost_estimate=pl.CostEstimate(
            flops=6 * rows * cols * depth * count, bytes_accessed=4 * (vectors.size + columns.size), transcendentals=0
        ),
        name="update",
    )(vectors, columns, diagonal, rows_hi, rows_lo, scaling)


def local(vectors, columns, diagonal, orbitals, pivots):
    depth = vectors.shape[2]
    count = pivots.shape[0]
    core = lax.axis_index("c")
    me = lax.axis_index(("y", "zh", "c", "zl", "x")).reshape(1)
    near = exchange(pick(me, pivots, diagonal, vectors), PEERS)

    own_chip, own_core = (pivots >> 17) * 8 + ((pivots & 1023) >> 7), (pivots >> 16) & 1
    block = own_chip * 2 + own_core
    order = jnp.arange(count)
    rank = jnp.sum((block[None, :] == block[:, None]) & (order[None, :] < order[:, None]), axis=1)
    place = jnp.where(own_core == core, own_chip * SLOTS + rank, -1)
    other = jnp.where(own_core == core, -1, own_chip * SLOTS + rank)
    slot = jnp.arange(64 * SLOTS)
    near_hot = (place[:, None] == slot[None, :]).astype(bf16)
    far_hot = (other[:, None] == slot[None, :]).astype(bf16)

    mine_v = transform(me, orbitals, vectors, False)
    got_v = sibling(mine_v)
    mine_c = transform(me, orbitals, columns, True)
    got_c = sibling(lax.dynamic_index_in_dim(mine_c, 1 - core, 0, False))
    chip_v = mine_v + got_v
    upper_v = lax.reduce_precision(chip_v, 8, 7)
    lower_v = (chip_v - upper_v).astype(bf16)
    upper_v = upper_v.astype(bf16)

    far = sibling(near)
    flat = (64 * SLOTS, depth + LANES)
    part, rows_hi, rows_lo, scaling = choose(
        me, near_hot, far_hot, near.reshape(flat), far.reshape(flat), upper_v, lower_v, mine_c, got_c
    )
    arrived = exchange(part, PEERS).reshape(64, 2, -1)
    updated = update(vectors, columns, diagonal, rows_hi, rows_lo, scaling)
    return arrived.sum(axis=0), updated


def solution(mesh):
    fine = Mesh(mesh.devices.reshape(4, 2, 2, 2, 4), ("y", "zh", "c", "zl", "x"))
    mu, nu = ("y", "zh", "c"), ("zl", "x")
    placed = (P(mu, nu, None), P(mu, nu, None), P(mu, nu), P(), P())
    return jax.shard_map(
        local,
        mesh=fine,
        in_specs=placed,
        out_specs=(P(mu + nu, None), P(mu, nu)),
        check_vma=False,
    )
```

profile of v0, /device:TPU:1, one launch (start us, length us, event | category | flops | bytes accessed | tf_op | source)
XLA Modules:
  0.0 74.9 jit_solution(2248256679426595075)
XLA Ops:
  0.6 4.2 %pick.1 = f32[64,8,640]{2,1,0:T(8,128)} custom-call(s32[1]{0:T(128)} %bitcast.me, s32[256]{0:T(256)} %pivots.1, f32[64,128]{1,0:T(8,128)} %diagonal.3, f32[64,128,512]{2,1,0:T(8,128)} %vectors.3), custom_call_target="tpu_custom_call" | custom-call | tf_op jit(solution)/shard_map/pick/pallas_call | solution.py:89
  4.9 0.0 copy-start.1
  4.9 12.0 %all-to-all-start = ((f32[64,8,640]{2,1,0:T(8,128)}), f32[64,8,640]{2,1,0:T(8,128)S(1)}, u32[]{:S(2)}, u32[]{:S(2)}) async-start(f32[64,8,640]{2,1,0:T(8,128)} %pick.1), calls=%async_computation | async-start | bytes 2621440 | tf_op jit(solution)/shard_map/all_to_all | solution.py:20
  16.9 0.0 copy-done.1
  17.0 0.2 copy.11.orbitals
  17.2 13.1 %turn_vectors.1 = f32[820,512]{1,0:T(8,128)} custom-call(s32[1]{0:T(128)} %bitcast.me, f32[1024,40]{1,0:T(8,128)S(1)} %copy.11.orbitals, f32[64,128,512]{2,1,0:T(8,128)} %vectors.3), custom_call_target="tpu_custom_call" | custom-call | flops 8053063680 | bytes 16777216 | tf_op jit(solution)/shard_map/turn_vectors/pallas_call | solution.py:167
  30.2 0.0 copy-start.2
  30.3 1.0 %collective-permute-start.1 = (f32[820,512]{1,0:T(8,128)}, f32[820,512]{1,0:T(8,128)}, u32[]{:S(2)}, u32[]{:S(2)}) collective-permute-start(f32[820,512]{1,0:T(8,128)} %turn_vectors.1), channel_id=1, source_target_pairs={{0,8},{8,0},{1,9},{9,1},{2,10},{10,2},{3,11},{11,3},{4,12},{12,4},... | collective-permute-start | bytes 5038088 | tf_op jit(solution)/shard_map/ppermute | solution.py:24
  31.3 5.8 %all-to-all-done = f32[64,8,640]{2,1,0:T(8,128)S(1)} async-done(((f32[64,8,640]{2,1,0:T(8,128)}), f32[64,8,640]{2,1,0:T(8,128)S(1)}, u32[]{:S(2)}, u32[]{:S(2)}) %all-to-all-start) | async-done | bytes 1310752 | tf_op jit(solution)/shard_map/all_to_all | solution.py:20
  37.1 2.5 %collective-permute-start = (f32[64,8,640]{2,1,0:T(8,128)S(1)}, f32[64,8,640]{2,1,0:T(8,128)}, u32[]{:S(2)}, u32[]{:S(2)}) collective-permute-start(f32[64,8,640]{2,1,0:T(8,128)S(1)} %all-to-all-done), channel_id=1, source_target_pairs={{0,8},{8,0},{1,9},{9,1},{2,10},{10,2},{3,11},{11,3},{4,12},{12,4},... | collective-permute-start | bytes 3932168 | tf_op jit(solution)/shard_map/ppermute | solution.py:24
  39.6 8.5 %turn_columns.1.mine_c = f32[2,128,820]{2,1,0:T(8,128)S(1)} custom-call(s32[1]{0:T(128)} %bitcast.me, f32[1024,40]{1,0:T(8,128)S(1)} %copy.11.orbitals, f32[64,128,256]{2,1,0:T(8,128)} %columns.1), custom_call_target="tpu_custom_call" | custom-call | flops 4026531840 | bytes 8388608 | tf_op jit(solution)/shard_map/turn_columns/pallas_call | solution.py:167
  48.2 0.1 collective-permute-start.2
  48.3 0.0 copy-done.2
  48.3 0.2 convert_reduce_fusion
  48.5 0.2 fusion.1
  48.7 0.0 collective-permute-done.1
  48.7 2.4 %fusion = (bf16[820,512]{1,0:T(8,128)(2,1)S(1)}, bf16[820,512]{1,0:T(8,128)(2,1)S(1)}) fusion(f32[820,512]{1,0:T(8,128)} %turn_vectors.1, f32[820,512]{1,0:T(8,128)} %collective-permute-done.1), kind=kLoop, calls=%fused_computation.2 | loop fusion | flops 2099200 | bytes 5038080 | tf_op jit(solution)/shard_map/convert_element_type | solution.py:293
  51.1 0.0 collective-permute-done.2.got_c
  51.1 0.0 collective-permute-done
  51.1 3.2 %choose.1 = (f32[128,820]{1,0:T(8,128)S(1)}, bf16[256,512]{1,0:T(8,128)(2,1)S(1)}, bf16[256,512]{1,0:T(8,128)(2,1)S(1)}, f32[8,256]{1,0:T(8,128)S(1)}) custom-call(s32[1]{0:T(128)} %bitcast.me, bf16[256,512]{1,0:T(8,128)(2,1)S(1)} %get-tuple-element.14.near_hot, bf16[256,512]{1,0:T(8,128)(2,1)S(1)} %get-tuple-element.15.far_hot, f32[512,640]{1,0:T(8,128)S(1)} %bitcast.5, ...), custom_call_target="tpu_custom_call" | custom-call | flops 2000000000 | bytes 6000000 | tf_op jit(solution)/shard_map/choose/pallas_call | solution.py:217
  54.3 0.0 copy-start
  54.4 1.0 %all_to_all.10 = f32[64,2,820]{2,1,0:T(2,128)} reshape(f32[128,820]{1,0:T(8,128)S(1)} %get-tuple-element.6) | data formatting | bytes 839680 | tf_op jit(solution)/shard_map/all_to_all | solution.py:20
  55.4 4.6 %all-to-all-start.1 = ((f32[64,2,820]{2,1,0:T(2,128)}), f32[64,2,820]{2,1,0:T(2,128)S(1)}, u32[]{:S(2)}, u32[]{:S(2)}) async-start(f32[64,2,820]{2,1,0:T(2,128)} %all_to_all.10), calls=%async_computation.1 | async-start | bytes 917504 | tf_op jit(solution)/shard_map/all_to_all | solution.py:20
  60.0 0.0 copy-done
  60.0 14.1 %update.1 = f32[64,128]{1,0:T(8,128)} custom-call(f32[64,128,512]{2,1,0:T(8,128)} %vectors.3, f32[64,128,256]{2,1,0:T(8,128)} %columns.1, f32[64,128]{1,0:T(8,128)S(1)} %copy-done, bf16[256,512]{1,0:T(8,128)(2,1)S(1)} %get-tuple-element.7.rows_hi, bf16[256,512]{1,0:T(8,128)(2,1)S(1)} %get-tuple-element.8.rows_lo, f32[8,256]{1,0:T(8,128)S(1)} %get-tuple-element.9.scaling), custom_call_target="tpu_custom_call" | custom-call | flops 6442450944 | bytes 25165824 | tf_op jit(solution)/shard_map/update/pallas_call | solution.py:249
  74.1 0.0 all-to-all-done.1
  74.1 0.8 %reduce_sum.19 = f32[2,820]{1,0:T(2,128)} reduce(f32[64,2,820]{2,1,0:T(2,128)S(1)} %all-to-all-done.1, f32[]{:T(128)} %constant.52.clone.1), dimensions={0}, to_apply=%region_1.2 | reduce | flops 103320 | bytes 426404 | tf_op jit(solution)/shard_map/reduce_sum | solution.py:303
  (3 shorter events, 0.1 us)
Async XLA Ops:
  4.9 12.1 %copy-start.1 = (f32[1024,40]{0,1:T(8,128)S(1)}, f32[1024,40]{0,1:T(8,128)}, u32[]{:S(2)}) copy-start(f32[1024,40]{0,1:T(8,128)} %param.8) | copy-start | bytes 491524
  4.9 32.2 %all-to-all-start = ((f32[64,8,640]{2,1,0:T(8,128)}), f32[64,8,640]{2,1,0:T(8,128)S(1)}, u32[]{:S(2)}, u32[]{:S(2)}) async-start(f32[64,8,640]{2,1,0:T(8,128)} %pick.1), calls=%async_computation | async-start | bytes 2621440 | tf_op jit(solution)/shard_map/all_to_all | solution.py:20
  30.2 18.0 %copy-start.2 = (s32[256]{0:T(256)S(1)}, s32[256]{0:T(256)}, u32[]{:S(2)}) copy-start(s32[256]{0:T(256)} %pivots.1) | copy-start | bytes 3076
  30.3 18.4 %collective-permute-start.1 = (f32[820,512]{1,0:T(8,128)}, f32[820,512]{1,0:T(8,128)}, u32[]{:S(2)}, u32[]{:S(2)}) collective-permute-start(f32[820,512]{1,0:T(8,128)} %turn_vectors.1), channel_id=1, source_target_pairs={{0,8},{8,0},{1,9},{9,1},{2,10},{10,2},{3,11},{11,3},{4,12},{12,4},... | collective-permute-start | bytes 5038088 | tf_op jit(solution)/shard_map/ppermute | solution.py:24
  37.1 14.0 %collective-permute-start = (f32[64,8,640]{2,1,0:T(8,128)S(1)}, f32[64,8,640]{2,1,0:T(8,128)}, u32[]{:S(2)}, u32[]{:S(2)}) collective-permute-start(f32[64,8,640]{2,1,0:T(8,128)S(1)} %all-to-all-done), channel_id=1, source_target_pairs={{0,8},{8,0},{1,9},{9,1},{2,10},{10,2},{3,11},{11,3},{4,12},{12,4},... | collective-permute-start | bytes 3932168 | tf_op jit(solution)/shard_map/ppermute | solution.py:24
  48.2 2.9 %collective-permute-start.2 = (f32[128,820]{1,0:T(8,128)S(1)}, f32[128,820]{1,0:T(8,128)S(1)}, u32[]{:S(2)}, u32[]{:S(2)}) collective-permute-start(f32[128,820]{1,0:T(8,128)S(1)} %dynamic-slice_bitcast_fusion), channel_id=1, source_target_pairs={{0,8},{8,0},{1,9},{9,1},{2,10},{10,2},{3,11},{11,3},{4,12},{12,4},... | collective-permute-start | bytes 1259528 | tf_op jit(solution)/shard_map/ppermute | solution.py:24
  54.3 5.7 %copy-start = (f32[64,128]{1,0:T(8,128)S(1)}, f32[64,128]{1,0:T(8,128)}, u32[]{:S(2)}) copy-start(f32[64,128]{1,0:T(8,128)} %diagonal.3) | copy-start | bytes 98308
  55.4 18.7 %all-to-all-start.1 = ((f32[64,2,820]{2,1,0:T(2,128)}), f32[64,2,820]{2,1,0:T(2,128)S(1)}, u32[]{:S(2)}, u32[]{:S(2)}) async-start(f32[64,2,820]{2,1,0:T(2,128)} %all_to_all.10), calls=%async_computation.1 | async-start | bytes 917504 | tf_op jit(solution)/shard_map/all_to_all | solution.py:20
where the time goes:
time: 75.6 us; the launch traced here: 74.9 us
  Pallas kernels  43.1 us (57%)
  starting transfers between devices  20.3 us (27%)
  waiting for transfers between devices  5.84 us (8%)
  other arithmetic  3.55 us (5%)
  local copies, waits for them, and re-layouts  1.28 us (2%)
  between operations  0.8 us (1%)
    pallas_call x2, Pallas kernels, transform(): pl.pallas_call(functools.partial(transform_kernel, flip), out_shape=jax.S...  21.6 us
    all_to_all x2, starting transfers between devices, exchange(): return lax.all_to_all(value, axes, split_axis=0, concat_axis=0, tiled=True)  16.7 us
    pallas_call x1, Pallas kernels, update(): pl.pallas_call(update_kernel, out_shape=jax.ShapeDtypeStruct((rows, cols)...  14.1 us
    all_to_all x2, waiting for transfers between devices, exchange(): return lax.all_to_all(value, axes, split_axis=0, concat_axis=0, tiled=True)  5.83 us
    pallas_call x1, Pallas kernels, pick(): pl.pallas_call(pick_kernel, out_shape=jax.ShapeDtypeStruct((64, SLOTS, de...  4.23 us
    ppermute x3, starting transfers between devices, sibling(): return lax.ppermute(value, 'c', [(0, 1), (1, 0)])  3.62 us
    pallas_call x1, Pallas kernels, choose(): pl.pallas_call(choose_kernel, out_shape=(jax.ShapeDtypeStruct((count // 2...  3.21 us
    convert_element_type x1, other arithmetic, local(): lower_v = (chip_v - upper_v).astype(bf16)  2.42 us
  transfers between devices with their start and end apart: 5, of which 1 were waited for; matrix products, arithmetic and copies ran while one was open for 4% of the time, Pallas kernels for 48%

commit v1 on v0

--- a/solution.py
+++ b/solution.py
@@ -50,14 +50,18 @@
     cols, depth = vectors.shape[1:]
     for slot in range(2 * SLOTS):
         index[slot] = 0
-
-    def scan(j, found):
-        pair = pivots[j]
-        index[found] = ((pair >> 10) & 63) * cols + (pair & 127)
-        owner = (pair >> 16) * 8 + ((pair & 1023) >> 7)
-        return found + (owner == me[0]).astype(jnp.int32)
-
-    found = lax.fori_loop(0, count, scan, 0, unroll=8)
+    key = (me[0] >> 3) * 65536 + (me[0] & 7) * LANES
+    group = 16
+
+    def scan(i, found):
+        pairs = [pivots[i * group + j] for j in range(group)]
+        owned = [((pair & 0xF0380) == key).astype(jnp.int32) for pair in pairs]
+        for pair, own in zip(pairs, owned):
+            index[found] = ((pair >> 10) & 63) * cols + (pair & 127)
+            found = found + own
+        return found
+
+    found = lax.fori_loop(0, count // group, scan, 0)
     copies = []
     for slot in range(SLOTS):
         spot = index[slot]
@@ -101,86 +105,92 @@
     )(me, pivots, diagonal, vectors)
 
 
-def transform_kernel(flip, me, orbitals, value, out, wide_hi, wide_lo, right2, half, square, *flat):
-    step = pl.program_id(0)
-    tall, cols, width = value.shape
-    rows = half.shape[0]
-    active = orbitals.shape[1]
-
-    @pl.when(step == 0)
-    def _():
-        left = orbitals[pl.ds(pl.multiple_of((me[0] >> 3) * rows, rows), rows), :]
-        right = orbitals[pl.ds(pl.multiple_of((me[0] & 7) * cols, cols), cols), :]
-        high = (active * 8, active)
-        spread_rows = jnp.where(iota(high, 0) // 8 == iota(high, 1), 1.0, 0.0).astype(bf16)
-        long = (rows, rows * 8)
-        spread_cols = jnp.where(iota(long, 0) == iota(long, 1) // 8, 1.0, 0.0).astype(bf16)
-        full = (active * 8, rows * 8)
-        same = iota(full, 0) % 8 == iota(full, 1) % 8
-        for part, wide in zip(split(left), (wide_hi, wide_lo)):
-            repeated = dot(dot_nt(spread_rows, part).astype(bf16), spread_cols)
-            wide[...] = jnp.where(same, repeated, 0.0).astype(bf16)
-        eye = jnp.where(iota((48, active), 0) == iota((48, active), 1), 1.0, 0.0).astype(bf16)
-        upper, lower = [dot_nt(eye, part).astype(bf16) for part in split(right)]
-        right2[:48, :cols] = upper
-        right2[:48, cols:] = upper
-        right2[48:, :cols] = lower
-        right2[48:, cols:] = jnp.zeros_like(lower)
-
-    for i in range(tall):
-        both = dot(right2[...], jnp.concatenate(split(value[i]), axis=0))
-        half[step * tall + i] = both[:active] + both[48 : 48 + active]
-
+def transform_kernel(flip, me, turned_orbitals, value, out, block, wide_hi, wide_lo, right2, half, square, sems, *flat):
+    rows, cols, width = block.shape
+    active = turned_orbitals.shape[0]
+    steps = sems.shape[0]
+    tall = rows // steps
+
+    def fetch(step):
+        part = pl.ds(step * tall, tall)
+        return pltpu.make_async_copy(value.at[part], block.at[part], sems.at[step])
+
+    for step in range(steps):
+        fetch(step).start()
+
+    index_mu = me[0] >> 3
+    left = turned_orbitals[:, pl.ds(pl.multiple_of((index_mu >> 1) * LANES, LANES), LANES)]
+    right = turned_orbitals[:, pl.ds(pl.multiple_of((me[0] & 7) * cols, cols), cols)]
+    high = (active * 8, active)
+    spread_rows = jnp.where(iota(high, 0) // 8 == iota(high, 1), 1.0, 0.0).astype(bf16)
+    long = (LANES, rows * 8)
+    spread_cols = jnp.where(iota(long, 0) == iota(long, 1) // 8 + (index_mu & 1) * rows, 1.0, 0.0).astype(bf16)
+    full = (active * 8, rows * 8)
+    same = iota(full, 0) % 8 == iota(full, 1) % 8
+    for part, wide in zip(split(left), (wide_hi, wide_lo)):
+        repeated = dot(dot(spread_rows, part).astype(bf16), spread_cols)
+        wide[...] = jnp.where(same, repeated, 0.0).astype(bf16)
+    eye = jnp.where(iota((48, active), 0) == iota((48, active), 1), 1.0, 0.0).astype(bf16)
+    upper, lower = [dot(eye, part).astype(bf16) for part in split(right)]
+    right2[:48, :cols] = upper
+    right2[:48, cols:] = upper
+    right2[48:, :cols] = lower
+    right2[48:, cols:] = jnp.zeros_like(lower)
+
+    def advance(step, carry):
+        fetch(step).wait()
+        for i in range(tall):
+            row = step * tall + i
+            both = dot(right2[...], jnp.concatenate(split(block[row]), axis=0))
+            half[row] = both[:active] + both[48 : 48 + active]
+        return carry
+
+    lax.fori_loop(0, steps, advance, 0)
     target = flat[0] if flip else out
-
-    @pl.when(step == pl.num_programs(0) - 1)
-    def _():
-        for q in range(0, active, 8):
-            upper, lower = split(half[:, q : q + 8, :].reshape(rows * 8, width))
-            hi, lo = wide_hi[8 * q :, :], wide_lo[8 * q :, :]
-            part = dot(hi, upper) + dot(lo, upper) + dot(hi, lower)
-            square[q:, q : q + 8, :] = part.reshape(active - q, 8, width)
-        for p in range(active):
-            target[p * (p + 1) // 2 : (p + 1) * (p + 2) // 2, :] = square[p, : p + 1, :]
-        if flip:
-            turned = target[...].T[:, : out.shape[2]]
-            for i in range(8):
-                for c in range(2):
-                    out[c, 16 * i : 16 * i + 16, :] = turned[32 * i + 16 * c : 32 * i + 16 * c + 16, :]
-
-
-def transform(me, orbitals, value, flip):
+    for q in range(0, active, 8):
+        upper, lower = split(half[:, q : q + 8, :].reshape(rows * 8, width))
+        hi, lo = wide_hi[8 * q :, :], wide_lo[8 * q :, :]
+        both = dot(jnp.concatenate([hi, lo], axis=0), upper)
+        part = both[: 8 * (active - q)] + both[8 * (active - q) :] + dot(hi, lower)
+        square[q:, q : q + 8, :] = part.reshape(active - q, 8, width)
+    for p in range(active):
+        target[p * (p + 1) // 2 : (p + 1) * (p + 2) // 2, :] = square[p, : p + 1, :]
+    if flip:
+        turned = target[...].T[:, : out.shape[2]]
+        for i in range(8):
+            for c in range(2):
+                out[c, 16 * i : 16 * i + 16, :] = turned[32 * i + 16 * c : 32 * i + 16 * c + 16, :]
+
+
+def transform(me, turned_orbitals, value, flip):
     rows, cols, width = value.shape
-    active = orbitals.shape[1]
+    active = turned_orbitals.shape[0]
     pairs = active * (active + 1) // 2
-    tall = 8
+    steps = 8
     shape = (2, width // 2, pairs) if flip else (pairs, width)
     scratch = [
+        pltpu.VMEM(value.shape, f32),
         pltpu.VMEM((active * 8, rows * 8), bf16),
         pltpu.VMEM((active * 8, rows * 8), bf16),
         pltpu.VMEM((96, 2 * cols), bf16),
         pltpu.VMEM((rows, active, width), f32),
         pltpu.VMEM((active, active, width), f32),
+        pltpu.SemaphoreType.DMA((steps,)),
     ]
     if flip:
         scratch.append(pltpu.VMEM((pl.cdiv(pairs, LANES) * LANES, width), f32))
     return pl.pallas_call(
         functools.partial(transform_kernel, flip),
         out_shape=jax.ShapeDtypeStruct(shape, f32),
-        grid=(rows // tall,),
-        in_specs=[
-            smem,
-            pl.BlockSpec(orbitals.shape, lambda i: (0, 0)),
-            pl.BlockSpec((tall, cols, width), lambda i: (i, 0, 0)),
-        ],
-        out_specs=pl.BlockSpec(shape, lambda i: (0,) * len(shape)),
+        in_specs=[smem, vmem, hbm],
+        out_specs=vmem,
         scratch_shapes=scratch,
-        compiler_params=params(52),
+        compiler_params=params(56),
         cost_estimate=pl.CostEstimate(
             flops=6 * active * 8 * rows * 8 * width * 16, bytes_accessed=value.size * 4, transcendentals=0
         ),
         name="turn_columns" if flip else "turn_vectors",
-    )(me, orbitals, value)
+    )(me, turned_orbitals, value)
 
 
 def choose_kernel(me, near_hot, far_hot, near, far, upper_v, lower_v, mine_c, got_c, part, rows_hi, rows_lo, scaling, keep_hi, keep_lo):
@@ -231,35 +241,53 @@
     )(me, near_hot, far_hot, near, far, upper_v, lower_v, mine_c, got_c)
 
 
-def update_kernel(vectors, columns, diagonal, rows_hi, rows_lo, scaling, out):
-    tall, cols, depth = vectors.shape
-    count = columns.shape[2]
-    upper, lower = split(vectors[...].reshape(tall * cols, depth))
-    update = dot_nt(upper, rows_hi[...]) + dot_nt(lower, rows_hi[...]) + dot_nt(upper, rows_lo[...])
-    fresh = (columns[...].reshape(tall * cols, count) - update) * scaling[:1, :]
-    square = fresh * fresh
-    folded = (square[:, :LANES] + square[:, LANES:]).reshape(tall, cols, LANES)
-    out[...] = diagonal[...] - jnp.sum(jnp.swapaxes(folded, 1, 2), axis=1)
+def update_kernel(vectors, columns, diagonal, rows_hi, rows_lo, scaling, out, block, beside, sems):
+    rows, cols, depth = block.shape
+    count = beside.shape[2]
+    steps = sems.shape[1]
+    tall = rows // steps
+
+    def fetch(step):
+        part = pl.ds(step * tall, tall)
+        return (
+            pltpu.make_async_copy(vectors.at[part], block.at[part], sems.at[0, step]),
+            pltpu.make_async_copy(columns.at[part], beside.at[part], sems.at[1, step]),
+        )
+
+    for step in range(steps):
+        for copy in fetch(step):
+            copy.start()
+
+    def advance(step, carry):
+        for copy in fetch(step):
+            copy.wait()
+        part = pl.ds(pl.multiple_of(step * tall, tall), tall)
+        upper, lower = split(block[part].reshape(tall * cols, depth))
+        update = dot_nt(upper, rows_hi[...]) + dot_nt(lower, rows_hi[...]) + dot_nt(upper, rows_lo[...])
+        fresh = (beside[part].reshape(tall * cols, count) - update) * scaling[:1, :]
+        square = fresh * fresh
+        folded = (square[:, :LANES] + square[:, LANES:]).reshape(tall, cols, LANES)
+        out[part, :] = diagonal[part, :] - jnp.sum(jnp.swapaxes(folded, 1, 2), axis=1)
+        return carry
+
+    lax.fori_loop(0, steps, advance, 0)
 
 
 def update(vectors, columns, diagonal, rows_hi, rows_lo, scaling):
     rows, cols, depth = vectors.shape
     count = columns.shape[2]
-    tall = 8
+    steps = 8
     return pl.pallas_call(
         update_kernel,
         out_shape=jax.ShapeDtypeStruct((rows, cols), f32),
-        grid=(rows // tall,),
-        in_specs=[
-            pl.BlockSpec((tall, cols, depth), lambda i: (i, 0, 0)),
-            pl.BlockSpec((tall, cols, count), lambda i: (i, 0, 0)),
-            pl.BlockSpec((tall, cols), lambda i: (i, 0)),
-            pl.BlockSpec((count, depth), lambda i: (0, 0)),
-            pl.BlockSpec((count, depth), lambda i: (0, 0)),
-            pl.BlockSpec((8, count), lambda i: (0, 0)),
+        in_specs=[hbm, hbm, vmem, vmem, vmem, vmem],
+        out_specs=vmem,
+        scratch_shapes=[
+            pltpu.VMEM(vectors.shape, f32),
+            pltpu.VMEM(columns.shape, f32),
+            pltpu.SemaphoreType.DMA((2, steps)),
         ],
-        out_specs=pl.BlockSpec((tall, cols), lambda i: (i, 0)),
-        compiler_params=params(52),
+        compiler_params=params(56),
         cost_estimate=pl.CostEstimate(
             flops=6 * rows * cols * depth * count, bytes_accessed=4 * (vectors.size + columns.size), transcendentals=0
         ),
@@ -284,9 +312,11 @@
     near_hot = (place[:, None] == slot[None, :]).astype(bf16)
     far_hot = (other[:, None] == slot[None, :]).astype(bf16)
 
+    orbitals = orbitals.T
     mine_v = transform(me, orbitals, vectors, False)
     got_v = sibling(mine_v)
     mine_c = transform(me, orbitals, columns, True)
+    near, mine_c = lax.optimization_barrier((near, mine_c))
     got_c = sibling(lax.dynamic_index_in_dim(mine_c, 1 - core, 0, False))
     chip_v = mine_v + got_v
     upper_v = lax.reduce_precision(chip_v, 8, 7)

time: 75.6 us -> 68.8 us (0.910)
  Pallas kernels: 43.1 us -> 36 us
  waiting for transfers between devices: 5.84 us -> 1.88 us
  local copies, waits for them, and re-layouts: 1.28 us -> 4.08 us
  starting transfers between devices: 20.3 us -> 21.9 us
    pallas_call x2, Pallas kernels: 21.6 us -> 17.5 us  [transform(): pl.pallas_call(functools.partial(transform_kernel, flip), out_shape=jax.S...]
    all_to_all x2, waiting for transfers between devices: 5.83 us -> 1.87 us  [exchange(): return lax.all_to_all(value, axes, split_axis=0, concat_axis=0, tiled=True)]
    all_to_all x2, starting transfers between devices: 16.7 us -> 18.5 us  [exchange(): return lax.all_to_all(value, axes, split_axis=0, concat_axis=0, tiled=True)]
    unnamed x7 -> x10, local copies, waits for them, and re-layouts: 0.21 us -> 1.99 us
    pallas_call x1, Pallas kernels: 14.1 us -> 12.5 us  [update(): pl.pallas_call(update_kernel, out_shape=jax.ShapeDtypeStruct((rows, cols)...]
    pallas_call x1, Pallas kernels: 3.21 us -> 1.89 us  [choose(): pl.pallas_call(choose_kernel, out_shape=(jax.ShapeDtypeStruct((count // 2...]
    squeeze x1, local copies, waits for them, and re-layouts: 0.04 us -> 1.06 us  [local(): got_c = sibling(lax.dynamic_index_in_dim(mine_c, 1 - core, 0, False))]
  transfers between devices with their start and end apart: 5 -> 5, of which waited for: 1 -> 1; matrix products, arithmetic and copies ran while one was open for 4% -> 6% of each run, Pallas kernels for 48% -> 44%
where the time goes in v1:
time: 68.8 us; the launch traced here: 68.3 us
  Pallas kernels  36 us (52%)
  starting transfers between devices  21.9 us (32%)
  local copies, waits for them, and re-layouts  4.08 us (6%)
  other arithmetic  3.63 us (5%)
  waiting for transfers between devices  1.88 us (3%)
  between operations  0.79 us (1%)
    all_to_all x2, starting transfers between devices, exchange(): return lax.all_to_all(value, axes, split_axis=0, concat_axis=0, tiled=True)  18.5 us
    pallas_call x2, Pallas kernels, transform(): pl.pallas_call(functools.partial(transform_kernel, flip), out_shape=jax.S...  17.5 us
    pallas_call x1, Pallas kernels, update(): pl.pallas_call(update_kernel, out_shape=jax.ShapeDtypeStruct((rows, cols)...  12.5 us
    pallas_call x1, Pallas kernels, pick(): pl.pallas_call(pick_kernel, out_shape=jax.ShapeDtypeStruct((64, SLOTS, de...  4.12 us
    ppermute x3, starting transfers between devices, sibling(): return lax.ppermute(value, 'c', [(0, 1), (1, 0)])  3.41 us
    convert_element_type x1, other arithmetic, local(): lower_v = (chip_v - upper_v).astype(bf16)  2.49 us
    unnamed x10, local copies, waits for them, and re-layouts  1.99 us
    pallas_call x1, Pallas kernels, choose(): pl.pallas_call(choose_kernel, out_shape=(jax.ShapeDtypeStruct((count // 2...  1.89 us
  transfers between devices with their start and end apart: 5, of which 1 were waited for; matrix products, arithmetic and copies ran while one was open for 6% of the time, Pallas kernels for 44%

profile of v1, /device:TPU:1, one launch (start us, length us, event | category | flops | bytes accessed | tf_op | source)
XLA Modules:
  0.0 68.3 jit_solution(12857310445738591115)
XLA Ops:
  0.6 4.1 %pick.1 = f32[64,8,640]{2,1,0:T(8,128)} custom-call(s32[1]{0:T(128)} %bitcast.me, s32[256]{0:T(256)} %pivots.1, f32[64,128]{1,0:T(8,128)} %diagonal.3, f32[64,128,512]{2,1,0:T(8,128)} %vectors.3), custom_call_target="tpu_custom_call" | custom-call | tf_op jit(solution)/shard_map/pick/pallas_call | solution.py:93
  4.8 12.0 %all-to-all-start = ((f32[64,8,640]{2,1,0:T(8,128)}), f32[64,8,640]{2,1,0:T(8,128)S(1)}, u32[]{:S(2)}, u32[]{:S(2)}) async-start(f32[64,8,640]{2,1,0:T(8,128)} %pick.1), calls=%async_computation | async-start | bytes 2621440 | tf_op jit(solution)/shard_map/all_to_all | solution.py:20
  16.8 10.5 %turn_vectors.1 = f32[820,512]{1,0:T(8,128)} custom-call(s32[1]{0:T(128)} %bitcast.me, f32[40,1024]{1,0:T(8,128)} %bitcast.8, f32[64,128,512]{2,1,0:T(8,128)} %vectors.3), custom_call_target="tpu_custom_call" | custom-call | flops 8053063680 | bytes 16777216 | tf_op jit(solution)/shard_map/turn_vectors/pallas_call | solution.py:182
  27.3 0.0 copy-start.4
  27.3 1.0 %collective-permute-start.1 = (f32[820,512]{1,0:T(8,128)}, f32[820,512]{1,0:T(8,128)}, u32[]{:S(2)}, u32[]{:S(2)}) collective-permute-start(f32[820,512]{1,0:T(8,128)} %turn_vectors.1), channel_id=1, source_target_pairs={{0,8},{8,0},{1,9},{9,1},{2,10},{10,2},{3,11},{11,3},{4,12},{12,4},... | collective-permute-start | bytes 5038088 | tf_op jit(solution)/shard_map/ppermute | solution.py:24
  28.3 7.0 %turn_columns.1.mine_c = f32[2,128,820]{2,1,0:T(8,128)} custom-call(s32[1]{0:T(128)} %bitcast.me, f32[40,1024]{1,0:T(8,128)} %bitcast.9, f32[64,128,256]{2,1,0:T(8,128)} %columns.1), custom_call_target="tpu_custom_call" | custom-call | flops 4026531840 | bytes 8388608 | tf_op jit(solution)/shard_map/turn_columns/pallas_call | solution.py:182
  35.3 1.9 %all-to-all-done = f32[64,8,640]{2,1,0:T(8,128)S(1)} async-done(((f32[64,8,640]{2,1,0:T(8,128)}), f32[64,8,640]{2,1,0:T(8,128)S(1)}, u32[]{:S(2)}, u32[]{:S(2)}) %all-to-all-start) | async-done | bytes 1310752 | tf_op jit(solution)/shard_map/all_to_all | solution.py:20
  37.2 2.3 %collective-permute-start = (f32[64,8,640]{2,1,0:T(8,128)S(1)}, f32[64,8,640]{2,1,0:T(8,128)S(1)}, u32[]{:S(2)}, u32[]{:S(2)}) collective-permute-start(f32[64,8,640]{2,1,0:T(8,128)S(1)} %all-to-all-done), channel_id=1, source_target_pairs={{0,8},{8,0},{1,9},{9,1},{2,10},{10,2},{3,11},{11,3},{4,12},{12,4},... | collective-permute-start | bytes 3932168 | tf_op jit(solution)/shard_map/ppermute | solution.py:24
  39.5 0.0 copy-done.4
  39.5 0.2 convert_reduce_fusion
  39.7 1.1 %dynamic-slice_bitcast_fusion = f32[128,820]{1,0:T(8,128)S(1)} fusion(f32[2,128,820]{2,1,0:T(8,128)} %turn_columns.1.mine_c, s32[]{:T(128)S(6)} %select_n.14), kind=kLoop, calls=%fused_computation.7 | loop fusion | bytes 839684 | tf_op jit(solution)/shard_map/jit(dynamic_index_in_dim)/squeeze | solution.py:320
  40.8 0.1 collective-permute-start.2
  40.9 0.2 fusion.1
  41.0 0.0 copy-start.2
  41.0 0.0 collective-permute-done.1
  41.1 2.5 %fusion = (bf16[820,512]{1,0:T(8,128)(2,1)S(1)}, bf16[820,512]{1,0:T(8,128)(2,1)S(1)}) fusion(f32[820,512]{1,0:T(8,128)} %turn_vectors.1, f32[820,512]{1,0:T(8,128)} %collective-permute-done.1), kind=kLoop, calls=%fused_computation.2 | loop fusion | flops 2099200 | bytes 5038080 | tf_op jit(solution)/shard_map/convert_element_type | solution.py:323
  43.6 0.0 collective-permute-done.2.got_c
  43.6 0.0 collective-permute-done
  43.6 0.0 copy-done.2
  43.6 1.9 %choose.1 = (f32[128,820]{1,0:T(8,128)S(1)}, bf16[256,512]{1,0:T(8,128)(2,1)S(1)}, bf16[256,512]{1,0:T(8,128)(2,1)S(1)}, f32[8,256]{1,0:T(8,128)S(1)}) custom-call(s32[1]{0:T(128)} %bitcast.me, bf16[256,512]{1,0:T(8,128)(2,1)S(1)} %get-tuple-element.18.near_hot, bf16[256,512]{1,0:T(8,128)(2,1)S(1)} %get-tuple-element.19.far_hot, f32[512,640]{1,0:T(8,128)S(1)} %bitcast.6, ...), custom_call_target="tpu_custom_call" | custom-call | flops 2000000000 | bytes 6000000 | tf_op jit(solution)/shard_map/choose/pallas_call | solution.py:227
  45.5 0.0 copy-start
  45.5 0.7 %copy-done = bf16[256,512]{1,0:T(8,128)(2,1)} copy-done((bf16[256,512]{1,0:T(8,128)(2,1)}, bf16[256,512]{1,0:T(8,128)(2,1)S(1)}, u32[]{:S(2)}) %copy-start) | copy-done | bytes 262168
  46.2 0.0 copy-start.1
  46.2 0.7 %copy-done.1 = bf16[256,512]{1,0:T(8,128)(2,1)} copy-done((bf16[256,512]{1,0:T(8,128)(2,1)}, bf16[256,512]{1,0:T(8,128)(2,1)S(1)}, u32[]{:S(2)}) %copy-start.1) | copy-done | bytes 262168
  46.9 0.0 copy-start.3
  46.9 0.6 copy-done.3
  47.5 1.0 %all_to_all.10 = f32[64,2,820]{2,1,0:T(2,128)} reshape(f32[128,820]{1,0:T(8,128)S(1)} %get-tuple-element.10) | data formatting | bytes 839680 | tf_op jit(solution)/shard_map/all_to_all | solution.py:20
  48.5 6.4 %all-to-all-start.1 = ((f32[64,2,820]{2,1,0:T(2,128)}), f32[64,2,820]{2,1,0:T(2,128)S(1)}, u32[]{:S(2)}, u32[]{:S(2)}) async-start(f32[64,2,820]{2,1,0:T(2,128)} %all_to_all.10), calls=%async_computation.1 | async-start | bytes 917504 | tf_op jit(solution)/shard_map/all_to_all | solution.py:20
  54.9 12.5 %update.1 = f32[64,128]{1,0:T(8,128)} custom-call(f32[64,128,512]{2,1,0:T(8,128)} %vectors.3, f32[64,128,256]{2,1,0:T(8,128)} %columns.1, f32[64,128]{1,0:T(8,128)} %diagonal.3, bf16[256,512]{1,0:T(8,128)(2,1)} %copy-done, bf16[256,512]{1,0:T(8,128)(2,1)} %copy-done.1, f32[8,256]{1,0:T(8,128)} %copy-done.3), custom_call_target="tpu_custom_call" | custom-call | flops 6442450944 | bytes 25165824 | tf_op jit(solution)/shard_map/update/pallas_call | solution.py:280
  67.5 0.0 all-to-all-done.1
  67.5 0.8 %reduce_sum.19 = f32[2,820]{1,0:T(2,128)} reduce(f32[64,2,820]{2,1,0:T(2,128)S(1)} %all-to-all-done.1, f32[]{:T(128)} %constant.52.clone.1), dimensions={0}, to_apply=%region_1.2 | reduce | flops 103320 | bytes 426404 | tf_op jit(solution)/shard_map/reduce_sum | solution.py:333
  (2 shorter events, 0.0 us)
Async XLA Ops:
  4.8 32.4 %all-to-all-start = ((f32[64,8,640]{2,1,0:T(8,128)}), f32[64,8,640]{2,1,0:T(8,128)S(1)}, u32[]{:S(2)}, u32[]{:S(2)}) async-start(f32[64,8,640]{2,1,0:T(8,128)} %pick.1), calls=%async_computation | async-start | bytes 2621440 | tf_op jit(solution)/shard_map/all_to_all | solution.py:20
  27.3 12.2 %copy-start.4 = (s32[256]{0:T(256)S(1)}, s32[256]{0:T(256)}, u32[]{:S(2)}) copy-start(s32[256]{0:T(256)} %pivots.1) | copy-start | bytes 3076
  27.3 13.7 %collective-permute-start.1 = (f32[820,512]{1,0:T(8,128)}, f32[820,512]{1,0:T(8,128)}, u32[]{:S(2)}, u32[]{:S(2)}) collective-permute-start(f32[820,512]{1,0:T(8,128)} %turn_vectors.1), channel_id=1, source_target_pairs={{0,8},{8,0},{1,9},{9,1},{2,10},{10,2},{3,11},{11,3},{4,12},{12,4},... | collective-permute-start | bytes 5038088 | tf_op jit(solution)/shard_map/ppermute | solution.py:24
  37.2 6.4 %collective-permute-start = (f32[64,8,640]{2,1,0:T(8,128)S(1)}, f32[64,8,640]{2,1,0:T(8,128)S(1)}, u32[]{:S(2)}, u32[]{:S(2)}) collective-permute-start(f32[64,8,640]{2,1,0:T(8,128)S(1)} %all-to-all-done), channel_id=1, source_target_pairs={{0,8},{8,0},{1,9},{9,1},{2,10},{10,2},{3,11},{11,3},{4,12},{12,4},... | collective-permute-start | bytes 3932168 | tf_op jit(solution)/shard_map/ppermute | solution.py:24
  40.8 2.8 %collective-permute-start.2 = (f32[128,820]{1,0:T(8,128)S(1)}, f32[128,820]{1,0:T(8,128)S(1)}, u32[]{:S(2)}, u32[]{:S(2)}) collective-permute-start(f32[128,820]{1,0:T(8,128)S(1)} %dynamic-slice_bitcast_fusion), channel_id=1, source_target_pairs={{0,8},{8,0},{1,9},{9,1},{2,10},{10,2},{3,11},{11,3},{4,12},{12,4},... | collective-permute-start | bytes 1259528 | tf_op jit(solution)/shard_map/ppermute | solution.py:24
  41.0 2.5 %copy-start.2 = (f32[2,128,820]{2,1,0:T(8,128)S(1)}, f32[2,128,820]{2,1,0:T(8,128)}, u32[]{:S(2)}) copy-start(f32[2,128,820]{2,1,0:T(8,128)} %turn_columns.1.mine_c) | copy-start | bytes 2519044
  45.5 0.7 %copy-start = (bf16[256,512]{1,0:T(8,128)(2,1)}, bf16[256,512]{1,0:T(8,128)(2,1)S(1)}, u32[]{:S(2)}) copy-start(bf16[256,512]{1,0:T(8,128)(2,1)S(1)} %get-tuple-element.11.rows_hi) | copy-start | bytes 786436
  46.2 0.7 %copy-start.1 = (bf16[256,512]{1,0:T(8,128)(2,1)}, bf16[256,512]{1,0:T(8,128)(2,1)S(1)}, u32[]{:S(2)}) copy-start(bf16[256,512]{1,0:T(8,128)(2,1)S(1)} %get-tuple-element.12.rows_lo) | copy-start | bytes 786436
  46.9 0.6 copy-start.3
  48.5 19.0 %all-to-all-start.1 = ((f32[64,2,820]{2,1,0:T(2,128)}), f32[64,2,820]{2,1,0:T(2,128)S(1)}, u32[]{:S(2)}, u32[]{:S(2)}) async-start(f32[64,2,820]{2,1,0:T(2,128)} %all_to_all.10), calls=%async_computation.1 | async-start | bytes 917504 | tf_op jit(solution)/shard_map/all_to_all | solution.py:20

commit v2 on v1

--- a/solution.py
+++ b/solution.py
@@ -105,18 +105,22 @@
     )(me, pivots, diagonal, vectors)
 
 
-def transform_kernel(flip, me, turned_orbitals, value, out, block, wide_hi, wide_lo, right2, half, square, sems, *flat):
-    rows, cols, width = block.shape
-    active = turned_orbitals.shape[0]
-    steps = sems.shape[0]
+def turn_kernel(
+    me, turned_orbitals, vectors, columns, out, keep, give, block, beside, wide_hi, wide_lo, right2, half, square, flat, sems
+):
+    rows, cols, _ = block.shape
+    active, pairs = turned_orbitals.shape[0], out.shape[0]
+    steps = sems.shape[1]
     tall = rows // steps
 
-    def fetch(step):
+    def fetch(kind, step):
         part = pl.ds(step * tall, tall)
-        return pltpu.make_async_copy(value.at[part], block.at[part], sems.at[step])
-
-    for step in range(steps):
-        fetch(step).start()
+        source, target = ((vectors, block), (columns, beside))[kind]
+        return pltpu.make_async_copy(source.at[part], target.at[part], sems.at[kind, step])
+
+    for kind in range(2):
+        for step in range(steps):
+            fetch(kind, step).start()
 
     index_mu = me[0] >> 3
     left = turned_orbitals[:, pl.ds(pl.multiple_of((index_mu >> 1) * LANES, LANES), LANES)]
@@ -137,75 +141,90 @@
     right2[48:, :cols] = lower
     right2[48:, cols:] = jnp.zeros_like(lower)
 
-    def advance(step, carry):
-        fetch(step).wait()
-        for i in range(tall):
-            row = step * tall + i
-            both = dot(right2[...], jnp.concatenate(split(block[row]), axis=0))
-            half[row] = both[:active] + both[48 : 48 + active]
-        return carry
-
-    lax.fori_loop(0, steps, advance, 0)
-    target = flat[0] if flip else out
-    for q in range(0, active, 8):
-        upper, lower = split(half[:, q : q + 8, :].reshape(rows * 8, width))
-        hi, lo = wide_hi[8 * q :, :], wide_lo[8 * q :, :]
-        both = dot(jnp.concatenate([hi, lo], axis=0), upper)
-        part = both[: 8 * (active - q)] + both[8 * (active - q) :] + dot(hi, lower)
-        square[q:, q : q + 8, :] = part.reshape(active - q, 8, width)
-    for p in range(active):
-        target[p * (p + 1) // 2 : (p + 1) * (p + 2) // 2, :] = square[p, : p + 1, :]
-    if flip:
-        turned = target[...].T[:, : out.shape[2]]
-        for i in range(8):
-            for c in range(2):
-                out[c, 16 * i : 16 * i + 16, :] = turned[32 * i + 16 * c : 32 * i + 16 * c + 16, :]
-
-
-def transform(me, turned_orbitals, value, flip):
-    rows, cols, width = value.shape
+    for kind, (value, target) in enumerate(((block, out), (beside, flat))):
+        width = value.shape[2]
+
+        def advance(step, carry):
+            fetch(kind, step).wait()
+            for i in range(tall):
+                row = step * tall + i
+                both = dot(right2[...], jnp.concatenate(split(value[row]), axis=0))
+                half[row, :, :width] = both[:active] + both[48 : 48 + active]
+            return carry
+
+        lax.fori_loop(0, steps, advance, 0)
+        for q in range(0, active, 8):
+            upper, lower = split(half[:, q : q + 8, :width].reshape(rows * 8, width))
+            hi, lo = wide_hi[8 * q :, :], wide_lo[8 * q :, :]
+            both = dot(jnp.concatenate([hi, lo], axis=0), upper)
+            part = both[: 8 * (active - q)] + both[8 * (active - q) :] + dot(hi, lower)
+            square[q:, q : q + 8, :width] = part.reshape(active - q, 8, width)
+        for p in range(active):
+            target[p * (p + 1) // 2 : (p + 1) * (p + 2) // 2, :] = square[p, : p + 1, :width]
+
+    turned = flat[...].T[:, :pairs]
+    first = (index_mu & 1) == 0
+    for i in range(8):
+        a, b = turned[32 * i : 32 * i + 16], turned[32 * i + 16 : 32 * i + 32]
+        keep[16 * i : 16 * i + 16, :] = jnp.where(first, a, b)
+        give[16 * i : 16 * i + 16, :] = jnp.where(first, b, a)
+
+
+def turn(me, turned_orbitals, vectors, columns):
+    rows, cols, depth = vectors.shape
+    count = columns.shape[2]
     active = turned_orbitals.shape[0]
     pairs = active * (active + 1) // 2
     steps = 8
-    shape = (2, width // 2, pairs) if flip else (pairs, width)
-    scratch = [
-        pltpu.VMEM(value.shape, f32),
-        pltpu.VMEM((active * 8, rows * 8), bf16),
-        pltpu.VMEM((active * 8, rows * 8), bf16),
-        pltpu.VMEM((96, 2 * cols), bf16),
-        pltpu.VMEM((rows, active, width), f32),
-        pltpu.VMEM((active, active, width), f32),
-        pltpu.SemaphoreType.DMA((steps,)),
-    ]
-    if flip:
-        scratch.append(pltpu.VMEM((pl.cdiv(pairs, LANES) * LANES, width), f32))
     return pl.pallas_call(
-        functools.partial(transform_kernel, flip),
-        out_shape=jax.ShapeDtypeStruct(shape, f32),
-        in_specs=[smem, vmem, hbm],
-        out_specs=vmem,
-        scratch_shapes=scratch,
+        turn_kernel,
+        out_shape=(
+            jax.ShapeDtypeStruct((pairs, depth), f32),
+            jax.ShapeDtypeStruct((count // 2, pairs), f32),
+            jax.ShapeDtypeStruct((count // 2, pairs), f32),
+        ),
+        in_specs=[smem, vmem, hbm, hbm],
+        out_specs=(vmem,) * 3,
+        scratch_shapes=[
+            pltpu.VMEM(vectors.shape, f32),
+            pltpu.VMEM(columns.shape, f32),
+            pltpu.VMEM((active * 8, rows * 8), bf16),
+            pltpu.VMEM((active * 8, rows * 8), bf16),
+            pltpu.VMEM((96, 2 * cols), bf16),
+            pltpu.VMEM((rows, active, depth), f32),
+            pltpu.VMEM((active, active, depth), f32),
+            pltpu.VMEM((pl.cdiv(pairs, LANES) * LANES, count), f32),
+            pltpu.SemaphoreType.DMA((2, steps)),
+        ],
         compiler_params=params(56),
         cost_estimate=pl.CostEstimate(
-            flops=6 * active * 8 * rows * 8 * width * 16, bytes_accessed=value.size * 4, transcendentals=0
+            flops=10**10, bytes_accessed=4 * (vectors.size + columns.size), transcendentals=0
         ),
-        name="turn_columns" if flip else "turn_vectors",
-    )(me, turned_orbitals, value)
-
-
-def choose_kernel(me, near_hot, far_hot, near, far, upper_v, lower_v, mine_c, got_c, part, rows_hi, rows_lo, scaling, keep_hi, keep_lo):
+        name="turn",
+    )(me, turned_orbitals, vectors, columns)
+
+
+def choose_kernel(
+    me, near_hot, far_hot, near, far, upper_v, lower_v, mine_c, got_c, part, rows_out, scale_out, rows_all, scaling, keep_hi, keep_lo, sems
+):
     slots, width = near.shape
     depth = width - LANES
+    count = near_hot.shape[0]
     core = (me[0] >> 3) & 1
     near_hi, near_lo = split(near[...])
     far_hi, far_lo = split(far[...])
     hi = dot(near_hot[...], near_hi) + dot(far_hot[...], far_hi)
     lo = dot(near_hot[...], near_lo) + dot(far_hot[...], far_lo)
     hi16, lo16 = hi.astype(bf16), lo.astype(bf16)
-    rows_hi[...] = hi16[:, :depth]
-    rows_lo[...] = lo16[:, :depth]
-    scale = hi[:, depth:] + lo[:, depth:]
-    scaling[...] = scale.T[:8]
+    rows_all[:count, :] = hi16[:, :depth]
+    rows_all[count:, :] = lo16[:, :depth]
+    scaling[...] = (hi[:, depth:] + lo[:, depth:]).T[:8]
+    copies = [
+        pltpu.make_async_copy(rows_all, rows_out, sems.at[0]),
+        pltpu.make_async_copy(scaling, scale_out, sems.at[1]),
+    ]
+    for copy in copies:
+        copy.start()
     keep_hi[...] = hi16.reshape(keep_hi.shape)
     keep_lo[...] = lo16.reshape(keep_lo.shape)
     home_hi = keep_hi[:, core].reshape(-1, width)
@@ -216,7 +235,9 @@
         + dot_nt(home_hi[:, :depth], lower_v[...])
     )
     scale = home_hi[:, depth : depth + 1].astype(f32) + home_lo[:, depth : depth + 1].astype(f32)
-    part[...] = (mine_c[core] + got_c[...] - moved) * scale
+    part[...] = ((mine_c[...] + got_c[...] - moved) * scale).reshape(part.shape)
+    for copy in copies:
+        copy.wait()
 
 
 def choose(me, near_hot, far_hot, near, far, upper_v, lower_v, mine_c, got_c):
@@ -227,21 +248,26 @@
     return pl.pallas_call(
         choose_kernel,
         out_shape=(
-            jax.ShapeDtypeStruct((count // 2, pairs), f32),
-            jax.ShapeDtypeStruct((count, depth), bf16),
-            jax.ShapeDtypeStruct((count, depth), bf16),
-            jax.ShapeDtypeStruct((8, count), f32),
+            jax.ShapeDtypeStruct((64, count // 128, pairs), f32),
+            pltpu.HBM((2 * count, depth), bf16),
+            pltpu.HBM((8, count), f32),
         ),
         in_specs=[smem] + [vmem] * 8,
-        out_specs=(vmem,) * 4,
-        scratch_shapes=[pltpu.VMEM((8, 2, 16, width), bf16), pltpu.VMEM((8, 2, 16, width), bf16)],
+        out_specs=(vmem, pl.BlockSpec(memory_space=pltpu.HBM), pl.BlockSpec(memory_space=pltpu.HBM)),
+        scratch_shapes=[
+            pltpu.VMEM((2 * count, depth), bf16),
+            pltpu.VMEM((8, count), f32),
+            pltpu.VMEM((8, 2, 16, width), bf16),
+            pltpu.VMEM((8, 2, 16, width), bf16),
+            pltpu.SemaphoreType.DMA((2,)),
+        ],
         compiler_params=params(24),
         cost_estimate=pl.CostEstimate(flops=2 * 10**9, bytes_accessed=6 * 10**6, transcendentals=0),
         name="choose",
     )(me, near_hot, far_hot, near, far, upper_v, lower_v, mine_c, got_c)
 
 
-def update_kernel(vectors, columns, diagonal, rows_hi, rows_lo, scaling, out, block, beside, sems):
+def update_kernel(vectors, columns, diagonal, rows_all, scaling, out, block, beside, sems):
     rows, cols, depth = block.shape
     count = beside.shape[2]
     steps = sems.shape[1]
@@ -263,7 +289,8 @@
             copy.wait()
         part = pl.ds(pl.multiple_of(step * tall, tall), tall)
         upper, lower = split(block[part].reshape(tall * cols, depth))
-        update = dot_nt(upper, rows_hi[...]) + dot_nt(lower, rows_hi[...]) + dot_nt(upper, rows_lo[...])
+        both = dot_nt(upper, rows_all[...])
+        update = both[:, :count] + both[:, count:] + dot_nt(lower, rows_all[:count, :])
         fresh = (beside[part].reshape(tall * cols, count) - update) * scaling[:1, :]
         square = fresh * fresh
         folded = (square[:, :LANES] + square[:, LANES:]).reshape(tall, cols, LANES)
@@ -273,14 +300,14 @@
     lax.fori_loop(0, steps, advance, 0)
 
 
-def update(vectors, columns, diagonal, rows_hi, rows_lo, scaling):
+def update(vectors, columns, diagonal, rows_all, scaling):
     rows, cols, depth = vectors.shape
     count = columns.shape[2]
     steps = 8
     return pl.pallas_call(
         update_kernel,
         out_shape=jax.ShapeDtypeStruct((rows, cols), f32),
-        in_specs=[hbm, hbm, vmem, vmem, vmem, vmem],
+        in_specs=[hbm, hbm, vmem, vmem, vmem],
         out_specs=vmem,
         scratch_shapes=[
             pltpu.VMEM(vectors.shape, f32),
@@ -292,7 +319,7 @@
             flops=6 * rows * cols * depth * count, bytes_accessed=4 * (vectors.size + columns.size), transcendentals=0
         ),
         name="update",
-    )(vectors, columns, diagonal, rows_hi, rows_lo, scaling)
+    )(vectors, columns, diagonal, rows_all, scaling)
 
 
 def local(vectors, columns, diagonal, orbitals, pivots):
@@ -312,24 +339,21 @@
     near_hot = (place[:, None] == slot[None, :]).astype(bf16)
     far_hot = (other[:, None] == slot[None, :]).astype(bf16)
 
-    orbitals = orbitals.T
-    mine_v = transform(me, orbitals, vectors, False)
-    got_v = sibling(mine_v)
-    mine_c = transform(me, orbitals, columns, True)
-    near, mine_c = lax.optimization_barrier((near, mine_c))
-    got_c = sibling(lax.dynamic_index_in_dim(mine_c, 1 - core, 0, False))
+    mine_v, keep_c, give_c = turn(me, orbitals.T, vectors, columns)
+    got_v, got_c = sibling(mine_v), sibling(give_c)
     chip_v = mine_v + got_v
     upper_v = lax.reduce_precision(chip_v, 8, 7)
     lower_v = (chip_v - upper_v).astype(bf16)
     upper_v = upper_v.astype(bf16)
 
+    near, keep_c = lax.optimization_barrier((near, keep_c))
     far = sibling(near)
     flat = (64 * SLOTS, depth + LANES)
-    part, rows_hi, rows_lo, scaling = choose(
-        me, near_hot, far_hot, near.reshape(flat), far.reshape(flat), upper_v, lower_v, mine_c, got_c
+    part, rows_all, scaling = choose(
+        me, near_hot, far_hot, near.reshape(flat), far.reshape(flat), upper_v, lower_v, keep_c, got_c
     )
-    arrived = exchange(part, PEERS).reshape(64, 2, -1)
-    updated = update(vectors, columns, diagonal, rows_hi, rows_lo, scaling)
+    arrived = exchange(part, PEERS)
+    updated = update(vectors, columns, diagonal, rows_all, scaling)
     return arrived.sum(axis=0), updated
 
 

time: 68.8 us -> 64 us (0.930)
  waiting for transfers between devices: 1.88 us -> 6.49 us
  local copies, waits for them, and re-layouts: 4.08 us -> 0.01 us
  Pallas kernels: 36 us -> 33.2 us
  starting transfers between devices: 21.9 us -> 20 us
    all_to_all x2, waiting for transfers between devices: 1.87 us -> 5.45 us  [exchange(): return lax.all_to_all(value, axes, split_axis=0, concat_axis=0, tiled=True)]
    pallas_call x3 -> x2, Pallas kernels: 19.4 us -> 16.7 us  [the longest x1 13.9 us: turn(): pl.pallas_call(turn_kernel, out_shape=(jax.ShapeDtypeStruct((pairs, depth...]
    unnamed x10 -> x4, local copies, waits for them, and re-layouts: 1.99 us -> 0.01 us
    all_to_all x2, starting transfers between devices: 18.5 us -> 16.6 us  [exchange(): return lax.all_to_all(value, axes, split_axis=0, concat_axis=0, tiled=True)]
    squeeze x1 -> x0, local copies, waits for them, and re-layouts: 1.06 us -> none  [local(): got_c = sibling(lax.dynamic_index_in_dim(mine_c, 1 - core, 0, False))]
    ppermute x3, waiting for transfers between devices: 0.01 us -> 1.04 us  [sibling(): return lax.ppermute(value, 'c', [(0, 1), (1, 0)])]
    all_to_all x1 -> x0, local copies, waits for them, and re-layouts: 1.03 us -> none  [exchange(): return lax.all_to_all(value, axes, split_axis=0, concat_axis=0, tiled=True)]
  transfers between devices with their start and end apart: 5 -> 5, of which waited for: 1 -> 2; matrix products, arithmetic and copies ran while one was open for 6% -> 4% of each run, Pallas kernels for 44% -> 41%
where the time goes in v2:
time: 64 us; the launch traced here: 63.5 us
  Pallas kernels  33.2 us (52%)
  starting transfers between devices  20 us (31%)
  waiting for transfers between devices  6.49 us (10%)
  other arithmetic  3.1 us (5%)
  between operations  0.74 us (1%)
    all_to_all x2, starting transfers between devices, exchange(): return lax.all_to_all(value, axes, split_axis=0, concat_axis=0, tiled=True)  16.6 us
    pallas_call x1, Pallas kernels, turn(): pl.pallas_call(turn_kernel, out_shape=(jax.ShapeDtypeStruct((pairs, depth...  13.9 us
    pallas_call x1, Pallas kernels, update(): pl.pallas_call(update_kernel, out_shape=jax.ShapeDtypeStruct((rows, cols)...  12.4 us
    all_to_all x2, waiting for transfers between devices, exchange(): return lax.all_to_all(value, axes, split_axis=0, concat_axis=0, tiled=True)  5.45 us
    pallas_call x1, Pallas kernels, pick(): pl.pallas_call(pick_kernel, out_shape=jax.ShapeDtypeStruct((64, SLOTS, de...  4.09 us
    ppermute x3, starting transfers between devices, sibling(): return lax.ppermute(value, 'c', [(0, 1), (1, 0)])  3.32 us
    pallas_call x1, Pallas kernels, choose(): pl.pallas_call(choose_kernel, out_shape=(jax.ShapeDtypeStruct((64, count...  2.79 us
    convert_element_type x1, other arithmetic, local(): lower_v = (chip_v - upper_v).astype(bf16)  1.96 us
  transfers between devices with their start and end apart: 5, of which 2 were waited for; matrix products, arithmetic and copies ran while one was open for 4% of the time, Pallas kernels for 41%

profile of v2, /device:TPU:1, one launch (start us, length us, event | category | flops | bytes accessed | tf_op | source)
XLA Modules:
  0.0 63.5 jit_solution(3145404282628924515)
XLA Ops:
  0.6 4.1 %pick.1 = f32[64,8,640]{2,1,0:T(8,128)} custom-call(s32[1]{0:T(128)} %bitcast.me, s32[256]{0:T(256)} %pivots.1, f32[64,128]{1,0:T(8,128)} %diagonal.3, f32[64,128,512]{2,1,0:T(8,128)} %vectors.5), custom_call_target="tpu_custom_call" | custom-call | tf_op jit(solution)/shard_map/pick/pallas_call | solution.py:93
  4.7 12.0 %all-to-all-start = ((f32[64,8,640]{2,1,0:T(8,128)}), f32[64,8,640]{2,1,0:T(8,128)S(1)}, u32[]{:S(2)}, u32[]{:S(2)}) async-start(f32[64,8,640]{2,1,0:T(8,128)} %pick.1), calls=%async_computation | async-start | bytes 2621440 | tf_op jit(solution)/shard_map/all_to_all | solution.py:20
  16.8 0.0 copy-start.1
  16.8 13.9 %turn.1 = (f32[820,512]{1,0:T(8,128)}, f32[128,820]{1,0:T(8,128)}, f32[128,820]{1,0:T(8,128)}) custom-call(s32[1]{0:T(128)} %bitcast.me, f32[40,1024]{1,0:T(8,128)} %bitcast.6, f32[64,128,512]{2,1,0:T(8,128)} %vectors.5, f32[64,128,256]{2,1,0:T(8,128)} %columns.3), custom_call_target="tpu_custom_call" | custom-call | flops 10000000000 | bytes 25165824 | tf_op jit(solution)/shard_map/turn/pallas_call | solution.py:179
  30.7 1.0 %collective-permute-start.1 = (f32[820,512]{1,0:T(8,128)}, f32[820,512]{1,0:T(8,128)S(1)}, u32[]{:S(2)}, u32[]{:S(2)}) collective-permute-start(f32[820,512]{1,0:T(8,128)} %get-tuple-element.12), channel_id=1, source_target_pairs={{0,8},{8,0},{1,9},{9,1},{2,10},{10,2},{3,11},{11,3},{4,12},{12,4},... | collective-permute-start | bytes 5038088 | tf_op jit(solution)/shard_map/ppermute | solution.py:24
  31.7 5.4 %all-to-all-done = f32[64,8,640]{2,1,0:T(8,128)S(1)} async-done(((f32[64,8,640]{2,1,0:T(8,128)}), f32[64,8,640]{2,1,0:T(8,128)S(1)}, u32[]{:S(2)}, u32[]{:S(2)}) %all-to-all-start) | async-done | bytes 1310752 | tf_op jit(solution)/shard_map/all_to_all | solution.py:20
  37.1 2.3 %collective-permute-start = (f32[64,8,640]{2,1,0:T(8,128)S(1)}, f32[64,8,640]{2,1,0:T(8,128)S(1)}, u32[]{:S(2)}, u32[]{:S(2)}) collective-permute-start(f32[64,8,640]{2,1,0:T(8,128)S(1)} %all-to-all-done), channel_id=1, source_target_pairs={{0,8},{8,0},{1,9},{9,1},{2,10},{10,2},{3,11},{11,3},{4,12},{12,4},... | collective-permute-start | bytes 3932168 | tf_op jit(solution)/shard_map/ppermute | solution.py:24
  39.5 0.0 collective-permute-start.2
  39.5 0.0 copy-done.1
  39.5 0.2 convert_reduce_fusion
  39.7 0.2 fusion.1
  39.8 0.0 copy-start
  39.8 0.0 collective-permute-done.1
  39.9 2.0 %fusion = (bf16[820,512]{1,0:T(8,128)(2,1)S(1)}, bf16[820,512]{1,0:T(8,128)(2,1)S(1)}) fusion(f32[820,512]{1,0:T(8,128)} %get-tuple-element.12, f32[820,512]{1,0:T(8,128)S(1)} %collective-permute-done.1), kind=kLoop, calls=%fused_computation.2 | loop fusion | flops 2099200 | bytes 5038080 | tf_op jit(solution)/shard_map/convert_element_type | solution.py:346
  41.8 1.0 %collective-permute-done.2.got_c = f32[128,820]{1,0:T(8,128)S(1)} collective-permute-done((f32[128,820]{1,0:T(8,128)}, f32[128,820]{1,0:T(8,128)S(1)}, u32[]{:S(2)}, u32[]{:S(2)}) %collective-permute-start.2) | collective-permute-done | bytes 419872 | tf_op jit(solution)/shard_map/ppermute | solution.py:24
  42.9 0.0 collective-permute-done
  42.9 0.0 copy-done
  42.9 2.8 %choose.1 = (f32[64,2,820]{2,1,0:T(2,128)}, bf16[512,512]{1,0:T(8,128)(2,1)}, f32[8,256]{1,0:T(8,128)}) custom-call(s32[1]{0:T(128)} %bitcast.me, bf16[256,512]{1,0:T(8,128)(2,1)S(1)} %get-tuple-element.22.near_hot, bf16[256,512]{1,0:T(8,128)(2,1)S(1)} %get-tuple-element.23.far_hot, f32[512,640]{1,0:T(8,128)S(1)} %bitcast.4, f32[512,640]{1,0:T(8,128)S(1)} %bitcast.5, ...), custom_call_target="tpu_custom_call" | custom-call | flops 2000000000 | bytes 6000000 | tf_op jit(solution)/shard_map/choose/pallas_call | solution.py:248
  45.7 4.6 %all-to-all-start.1 = ((f32[64,2,820]{2,1,0:T(2,128)}), f32[64,2,820]{2,1,0:T(2,128)S(1)}, u32[]{:S(2)}, u32[]{:S(2)}) async-start(f32[64,2,820]{2,1,0:T(2,128)} %get-tuple-element.15), calls=%async_computation.1 | async-start | bytes 917504 | tf_op jit(solution)/shard_map/all_to_all | solution.py:20
  50.3 12.4 %update.1 = f32[64,128]{1,0:T(8,128)} custom-call(f32[64,128,512]{2,1,0:T(8,128)} %vectors.5, f32[64,128,256]{2,1,0:T(8,128)} %columns.3, f32[64,128]{1,0:T(8,128)} %diagonal.3, bf16[512,512]{1,0:T(8,128)(2,1)} %get-tuple-element.16.rows_all, f32[8,256]{1,0:T(8,128)} %get-tuple-element.17.scaling), custom_call_target="tpu_custom_call" | custom-call | flops 6442450944 | bytes 25165824 | tf_op jit(solution)/shard_map/update/pallas_call | solution.py:307
  62.7 0.0 all-to-all-done.1
  62.7 0.8 %reduce_sum.19 = f32[2,820]{1,0:T(2,128)} reduce(f32[64,2,820]{2,1,0:T(2,128)S(1)} %all-to-all-done.1, f32[]{:T(128)} %constant.45.clone.1), dimensions={0}, to_apply=%region_1.2 | reduce | flops 103320 | bytes 426404 | tf_op jit(solution)/shard_map/reduce_sum | solution.py:357
  (2 shorter events, 0.0 us)
Async XLA Ops:
  4.7 32.4 %all-to-all-start = ((f32[64,8,640]{2,1,0:T(8,128)}), f32[64,8,640]{2,1,0:T(8,128)S(1)}, u32[]{:S(2)}, u32[]{:S(2)}) async-start(f32[64,8,640]{2,1,0:T(8,128)} %pick.1), calls=%async_computation | async-start | bytes 2621440 | tf_op jit(solution)/shard_map/all_to_all | solution.py:20
  16.8 22.7 %copy-start.1 = (s32[256]{0:T(256)S(1)}, s32[256]{0:T(256)}, u32[]{:S(2)}) copy-start(s32[256]{0:T(256)} %pivots.1) | copy-start | bytes 3076
  30.7 9.2 %collective-permute-start.1 = (f32[820,512]{1,0:T(8,128)}, f32[820,512]{1,0:T(8,128)S(1)}, u32[]{:S(2)}, u32[]{:S(2)}) collective-permute-start(f32[820,512]{1,0:T(8,128)} %get-tuple-element.12), channel_id=1, source_target_pairs={{0,8},{8,0},{1,9},{9,1},{2,10},{10,2},{3,11},{11,3},{4,12},{12,4},... | collective-permute-start | bytes 5038088 | tf_op jit(solution)/shard_map/ppermute | solution.py:24
  37.1 5.7 %collective-permute-start = (f32[64,8,640]{2,1,0:T(8,128)S(1)}, f32[64,8,640]{2,1,0:T(8,128)S(1)}, u32[]{:S(2)}, u32[]{:S(2)}) collective-permute-start(f32[64,8,640]{2,1,0:T(8,128)S(1)} %all-to-all-done), channel_id=1, source_target_pairs={{0,8},{8,0},{1,9},{9,1},{2,10},{10,2},{3,11},{11,3},{4,12},{12,4},... | collective-permute-start | bytes 3932168 | tf_op jit(solution)/shard_map/ppermute | solution.py:24
  39.5 3.4 %collective-permute-start.2 = (f32[128,820]{1,0:T(8,128)}, f32[128,820]{1,0:T(8,128)S(1)}, u32[]{:S(2)}, u32[]{:S(2)}) collective-permute-start(f32[128,820]{1,0:T(8,128)} %get-tuple-element.14), channel_id=1, source_target_pairs={{0,8},{8,0},{1,9},{9,1},{2,10},{10,2},{3,11},{11,3},{4,12},{12,4},... | collective-permute-start | bytes 1259528 | tf_op jit(solution)/shard_map/ppermute | solution.py:24
  39.8 3.0 %copy-start = (f32[128,820]{1,0:T(8,128)S(1)}, f32[128,820]{1,0:T(8,128)}, u32[]{:S(2)}) copy-start(f32[128,820]{1,0:T(8,128)} %get-tuple-element.13.mine_c) | copy-start | bytes 1259524
  45.7 17.1 %all-to-all-start.1 = ((f32[64,2,820]{2,1,0:T(2,128)}), f32[64,2,820]{2,1,0:T(2,128)S(1)}, u32[]{:S(2)}, u32[]{:S(2)}) async-start(f32[64,2,820]{2,1,0:T(2,128)} %get-tuple-element.15), calls=%async_computation.1 | async-start | bytes 917504 | tf_op jit(solution)/shard_map/all_to_all | solution.py:20

commit v3 on v2

--- a/solution.py
+++ b/solution.py
@@ -8,6 +8,7 @@
 from jax.sharding import Mesh, PartitionSpec as P
 
 SLOTS = 8
+PER_ROW = 4
 LANES = 128
 PEERS = ("y", "zh", "zl", "x")
 f32, bf16 = jnp.float32, jnp.bfloat16
@@ -45,9 +46,9 @@
     return pltpu.CompilerParams(vmem_limit_bytes=mib << 20)
 
 
-def pick_kernel(me, pivots, diagonal, vectors, out, rows, spots, index, sems):
+def pick_kernel(me, pivots, diagonal, vectors, out, rows, spots, tile, index, sems):
     count = pivots.shape[0]
-    cols, depth = vectors.shape[1:]
+    depth = vectors.shape[2]
     for slot in range(2 * SLOTS):
         index[slot] = 0
     key = (me[0] >> 3) * 65536 + (me[0] & 7) * LANES
@@ -56,50 +57,59 @@
     def scan(i, found):
         pairs = [pivots[i * group + j] for j in range(group)]
         owned = [((pair & 0xF0380) == key).astype(jnp.int32) for pair in pairs]
-        for pair, own in zip(pairs, owned):
-            index[found] = ((pair >> 10) & 63) * cols + (pair & 127)
-            found = found + own
-        return found
+
+        def note(spot):
+            for pair, own in zip(pairs, owned):
+                index[spot] = pair
+                spot = spot + own
+            return spot
+
+        total = functools.reduce(lambda a, b: a | b, owned)
+        return lax.cond(total > 0, note, lambda spot: spot, found)
 
     found = lax.fori_loop(0, count // group, scan, 0)
     copies = []
     for slot in range(SLOTS):
-        spot = index[slot]
-        copies.append(
-            pltpu.make_async_copy(
-                vectors.at[spot >> 7, pl.ds(spot & 127, 1), :],
-                rows.at[pl.ds(slot, 1), :],
-                sems.at[slot],
-            )
-        )
-        copies[-1].start()
-    lane = iota((1, LANES), 1)
+        row, col = (index[slot] >> 10) & 63, index[slot] & 127
+        here = pl.ds(slot, 1)
+        copies.append(pltpu.make_async_copy(vectors.at[row, pl.ds(col, 1), :], rows.at[here, :], sems.at[0, slot]))
+        copies.append(pltpu.make_async_copy(diagonal.at[pl.ds(row, 1), :], spots.at[here, :], sems.at[1, slot]))
+    for copy in copies:
+        copy.start()
+    column = iota((SLOTS, 1), 0)
+    chosen = jnp.zeros((SLOTS, 1), jnp.int32)
     for slot in range(SLOTS):
-        spot = index[slot]
-        line = diagonal[pl.ds(spot >> 7, 1), :]
-        spots[pl.ds(slot, 1), :] = jnp.where(lane == (spot & 127), line, 0.0)
+        chosen = jnp.where(column == slot, index[slot] & 127, chosen)
     for copy in copies:
         copy.wait()
     used = iota((SLOTS, 1), 0) < found
     picked = jnp.where(used, rows[...], 0.0)
-    residual = jnp.sum(spots[...], axis=1, keepdims=True) - jnp.sum(picked * picked, axis=1, keepdims=True)
+    residual = jnp.sum(jnp.where(iota((SLOTS, LANES), 1) == chosen, spots[...], 0.0), axis=1, keepdims=True) - jnp.sum(picked * picked, axis=1, keepdims=True)
     scale = lax.rsqrt(jnp.maximum(jnp.where(used, residual, 1.0), 1.0))
-    out[:, :, :depth] = jnp.broadcast_to(picked[None], (64, SLOTS, depth))
-    out[:, :, depth:] = jnp.broadcast_to(scale[None], (64, SLOTS, LANES))
+    lane = iota((1, LANES), 1) // (LANES // PER_ROW)
+    for r in range(SLOTS // PER_ROW):
+        line = jnp.zeros((1, LANES), f32)
+        for i in range(PER_ROW):
+            slot = r * PER_ROW + i
+            tile[r : r + 1, depth * i : depth * (i + 1)] = picked[slot : slot + 1, :]
+            line = jnp.where(lane == i, scale[slot : slot + 1, :], line)
+        tile[r : r + 1, depth * PER_ROW :] = line
+    out[...] = jnp.broadcast_to(tile[...][None], out.shape)
 
 
 def pick(me, pivots, diagonal, vectors):
     depth = vectors.shape[2]
     return pl.pallas_call(
         pick_kernel,
-        out_shape=jax.ShapeDtypeStruct((64, SLOTS, depth + LANES), f32),
-        in_specs=[smem, smem, vmem, hbm],
+        out_shape=jax.ShapeDtypeStruct((64, SLOTS // PER_ROW, depth * PER_ROW + LANES), f32),
+        in_specs=[smem, smem, hbm, hbm],
         out_specs=vmem,
         scratch_shapes=[
             pltpu.VMEM((SLOTS, depth), f32),
             pltpu.VMEM((SLOTS, LANES), f32),
+            pltpu.VMEM((SLOTS // PER_ROW, depth * PER_ROW + LANES), f32),
             pltpu.SMEM((2 * SLOTS,), jnp.int32),
-            pltpu.SemaphoreType.DMA((SLOTS,)),
+            pltpu.SemaphoreType.DMA((2, SLOTS)),
         ],
         name="pick",
     )(me, pivots, diagonal, vectors)
@@ -204,15 +214,25 @@
     )(me, turned_orbitals, vectors, columns)
 
 
+def unpack(packed):
+    rows = packed.shape[0] * packed.shape[1]
+    depth = (packed.shape[2] - LANES) // PER_ROW
+    flat = packed[...].reshape(rows, packed.shape[2])
+    vectors = [flat[:, depth * i : depth * (i + 1)] for i in range(PER_ROW)]
+    spots = [depth * PER_ROW + LANES // PER_ROW * i for i in range(PER_ROW)]
+    scales = [jnp.broadcast_to(flat[:, spot : spot + 1], (rows, LANES)) for spot in spots]
+    return jnp.concatenate([jnp.concatenate(vectors, axis=0), jnp.concatenate(scales, axis=0)], axis=1)
+
+
 def choose_kernel(
     me, near_hot, far_hot, near, far, upper_v, lower_v, mine_c, got_c, part, rows_out, scale_out, rows_all, scaling, keep_hi, keep_lo, sems
 ):
-    slots, width = near.shape
-    depth = width - LANES
+    depth = rows_all.shape[1]
+    width = depth + LANES
     count = near_hot.shape[0]
     core = (me[0] >> 3) & 1
-    near_hi, near_lo = split(near[...])
-    far_hi, far_lo = split(far[...])
+    near_hi, near_lo = split(unpack(near))
+    far_hi, far_lo = split(unpack(far))
     hi = dot(near_hot[...], near_hi) + dot(far_hot[...], far_hi)
     lo = dot(near_hot[...], near_lo) + dot(far_hot[...], far_lo)
     hi16, lo16 = hi.astype(bf16), lo.astype(bf16)
@@ -242,8 +262,8 @@
 
 def choose(me, near_hot, far_hot, near, far, upper_v, lower_v, mine_c, got_c):
     count, slots = near_hot.shape
-    width = near.shape[1]
-    depth = width - LANES
+    depth = upper_v.shape[1]
+    width = depth + LANES
     pairs = upper_v.shape[0]
     return pl.pallas_call(
         choose_kernel,
@@ -323,7 +343,6 @@
 
 
 def local(vectors, columns, diagonal, orbitals, pivots):
-    depth = vectors.shape[2]
     count = pivots.shape[0]
     core = lax.axis_index("c")
     me = lax.axis_index(("y", "zh", "c", "zl", "x")).reshape(1)
@@ -333,8 +352,9 @@
     block = own_chip * 2 + own_core
     order = jnp.arange(count)
     rank = jnp.sum((block[None, :] == block[:, None]) & (order[None, :] < order[:, None]), axis=1)
-    place = jnp.where(own_core == core, own_chip * SLOTS + rank, -1)
-    other = jnp.where(own_core == core, -1, own_chip * SLOTS + rank)
+    spot = rank % PER_ROW * (64 * SLOTS // PER_ROW) + own_chip * (SLOTS // PER_ROW) + rank // PER_ROW
+    place = jnp.where(own_core == core, spot, -1)
+    other = jnp.where(own_core == core, -1, spot)
     slot = jnp.arange(64 * SLOTS)
     near_hot = (place[:, None] == slot[None, :]).astype(bf16)
     far_hot = (other[:, None] == slot[None, :]).astype(bf16)
@@ -348,10 +368,7 @@
 
     near, keep_c = lax.optimization_barrier((near, keep_c))
     far = sibling(near)
-    flat = (64 * SLOTS, depth + LANES)
-    part, rows_all, scaling = choose(
-        me, near_hot, far_hot, near.reshape(flat), far.reshape(flat), upper_v, lower_v, keep_c, got_c
-    )
+    part, rows_all, scaling = choose(me, near_hot, far_hot, near, far, upper_v, lower_v, keep_c, got_c)
     arrived = exchange(part, PEERS)
     updated = update(vectors, columns, diagonal, rows_all, scaling)
     return arrived.sum(axis=0), updated

time: 64 us -> 63.6 us (level)
  waiting for transfers between devices: 6.49 us -> 3.22 us
  starting transfers between devices: 20 us -> 22.9 us
    all_to_all x2, starting transfers between devices: 16.6 us -> 19.6 us  [exchange(): return lax.all_to_all(value, axes, split_axis=0, concat_axis=0, tiled=True)]
    all_to_all x2, waiting for transfers between devices: 5.45 us -> 3.09 us  [exchange(): return lax.all_to_all(value, axes, split_axis=0, concat_axis=0, tiled=True)]
    ppermute x3, waiting for transfers between devices: 1.04 us -> 0.13 us  [sibling(): return lax.ppermute(value, 'c', [(0, 1), (1, 0)])]
  transfers between devices with their start and end apart: 5 -> 5, of which waited for: 2 -> 2; matrix products, arithmetic and copies ran while one was open for 4% -> 4% of each run, Pallas kernels for 41% -> 42%
where the time goes in v3:
time: 63.6 us; the launch traced here: 63.2 us
  Pallas kernels  33.1 us (52%)
  starting transfers between devices  22.9 us (36%)
  waiting for transfers between devices  3.22 us (5%)
  other arithmetic  3.17 us (5%)
  between operations  0.76 us (1%)
    all_to_all x2, starting transfers between devices, exchange(): return lax.all_to_all(value, axes, split_axis=0, concat_axis=0, tiled=True)  19.6 us
    pallas_call x1, Pallas kernels, turn(): pl.pallas_call(turn_kernel, out_shape=(jax.ShapeDtypeStruct((pairs, depth...  13.9 us
    pallas_call x1, Pallas kernels, update(): pl.pallas_call(update_kernel, out_shape=jax.ShapeDtypeStruct((rows, cols)...  12.4 us
    pallas_call x1, Pallas kernels, pick(): pl.pallas_call(pick_kernel, out_shape=jax.ShapeDtypeStruct((64, SLOTS //...  3.76 us
    ppermute x3, starting transfers between devices, sibling(): return lax.ppermute(value, 'c', [(0, 1), (1, 0)])  3.36 us
    all_to_all x2, waiting for transfers between devices, exchange(): return lax.all_to_all(value, axes, split_axis=0, concat_axis=0, tiled=True)  3.09 us
    pallas_call x1, Pallas kernels, choose(): pl.pallas_call(choose_kernel, out_shape=(jax.ShapeDtypeStruct((64, count...  2.97 us
    convert_element_type x1, other arithmetic, local(): lower_v = (chip_v - upper_v).astype(bf16)  1.96 us
  transfers between devices with their start and end apart: 5, of which 2 were waited for; matrix products, arithmetic and copies ran while one was open for 4% of the time, Pallas kernels for 42%

profile of v3, /device:TPU:1, one launch (start us, length us, event | category | flops | bytes accessed | tf_op | source)
XLA Modules:
  0.0 63.2 jit_solution(6257152948362635966)
XLA Ops:
  0.6 3.8 %pick.1 = f32[64,2,2176]{2,1,0:T(2,128)} custom-call(s32[1]{0:T(128)} %bitcast.me, s32[256]{0:T(256)} %pivots.1, f32[64,128]{1,0:T(8,128)} %diagonal.3, f32[64,128,512]{2,1,0:T(8,128)} %vectors.5), custom_call_target="tpu_custom_call" | custom-call | tf_op jit(solution)/shard_map/pick/pallas_call | solution.py:102
  4.4 12.1 %all-to-all-start = ((f32[64,2,2176]{2,1,0:T(2,128)}), f32[64,2,2176]{2,1,0:T(2,128)S(1)}, u32[]{:S(2)}, u32[]{:S(2)}) async-start(f32[64,2,2176]{2,1,0:T(2,128)} %pick.1), calls=%async_computation | async-start | bytes 2228224 | tf_op jit(solution)/shard_map/all_to_all | solution.py:21
  16.5 0.0 copy-start.1
  16.5 13.9 %turn.1 = (f32[820,512]{1,0:T(8,128)}, f32[128,820]{1,0:T(8,128)}, f32[128,820]{1,0:T(8,128)}) custom-call(s32[1]{0:T(128)} %bitcast.me, f32[40,1024]{1,0:T(8,128)} %bitcast.2, f32[64,128,512]{2,1,0:T(8,128)} %vectors.5, f32[64,128,256]{2,1,0:T(8,128)} %columns.3), custom_call_target="tpu_custom_call" | custom-call | flops 10000000000 | bytes 25165824 | tf_op jit(solution)/shard_map/turn/pallas_call | solution.py:189
  30.5 1.0 %collective-permute-start.1 = (f32[820,512]{1,0:T(8,128)}, f32[820,512]{1,0:T(8,128)S(1)}, u32[]{:S(2)}, u32[]{:S(2)}) collective-permute-start(f32[820,512]{1,0:T(8,128)} %get-tuple-element.12), channel_id=1, source_target_pairs={{0,8},{8,0},{1,9},{9,1},{2,10},{10,2},{3,11},{11,3},{4,12},{12,4},... | collective-permute-start | bytes 5038088 | tf_op jit(solution)/shard_map/ppermute | solution.py:25
  31.5 0.1 collective-permute-start.2
  31.6 0.0 copy-done.1
  31.6 0.2 convert_reduce_fusion
  31.7 3.1 %all-to-all-done.near = f32[64,2,2176]{2,1,0:T(2,128)S(1)} async-done(((f32[64,2,2176]{2,1,0:T(2,128)}), f32[64,2,2176]{2,1,0:T(2,128)S(1)}, u32[]{:S(2)}, u32[]{:S(2)}) %all-to-all-start) | async-done | bytes 1114144 | tf_op jit(solution)/shard_map/all_to_all | solution.py:21
  34.8 2.3 %collective-permute-start = (f32[64,2,2176]{2,1,0:T(2,128)S(1)}, f32[64,2,2176]{2,1,0:T(2,128)S(1)}, u32[]{:S(2)}, u32[]{:S(2)}) collective-permute-start(f32[64,2,2176]{2,1,0:T(2,128)S(1)} %all-to-all-done.near), channel_id=1, source_target_pairs={{0,8},{8,0},{1,9},{9,1},{2,10},{10,2},{3,11},{11,3},{4,12},{12,4},... | collective-permute-start | bytes 3342344 | tf_op jit(solution)/shard_map/ppermute | solution.py:25
  37.1 0.1 fusion.1.near_hot
  37.3 0.1 fusion.2.far_hot
  37.4 0.0 copy-start
  37.4 0.0 collective-permute-done.1
  37.4 2.0 %fusion = (bf16[820,512]{1,0:T(8,128)(2,1)S(1)}, bf16[820,512]{1,0:T(8,128)(2,1)S(1)}) fusion(f32[820,512]{1,0:T(8,128)} %get-tuple-element.12, f32[820,512]{1,0:T(8,128)S(1)} %collective-permute-done.1), kind=kLoop, calls=%fused_computation.2 | loop fusion | flops 2099200 | bytes 5038080 | tf_op jit(solution)/shard_map/convert_element_type | solution.py:366
  39.4 0.0 collective-permute-done.2.got_c
  39.4 0.1 collective-permute-done.far
  39.5 0.0 copy-done
  39.5 3.0 %choose.1 = (f32[64,2,820]{2,1,0:T(2,128)}, bf16[512,512]{1,0:T(8,128)(2,1)}, f32[8,256]{1,0:T(8,128)}) custom-call(s32[1]{0:T(128)} %bitcast.me, bf16[256,512]{1,0:T(8,128)(2,1)S(1)} %fusion.1.near_hot, bf16[256,512]{1,0:T(8,128)(2,1)S(1)} %fusion.2.far_hot, f32[64,2,2176]{2,1,0:T(2,128)S(1)} %all-to-all-done.near, ...), custom_call_target="tpu_custom_call" | custom-call | flops 2000000000 | bytes 6000000 | tf_op jit(solution)/shard_map/choose/pallas_call | solution.py:268
  42.5 7.5 %all-to-all-start.1 = ((f32[64,2,820]{2,1,0:T(2,128)}), f32[64,2,820]{2,1,0:T(2,128)S(1)}, u32[]{:S(2)}, u32[]{:S(2)}) async-start(f32[64,2,820]{2,1,0:T(2,128)} %get-tuple-element.15), calls=%async_computation.1 | async-start | bytes 917504 | tf_op jit(solution)/shard_map/all_to_all | solution.py:21
  50.0 12.4 %update.1 = f32[64,128]{1,0:T(8,128)} custom-call(f32[64,128,512]{2,1,0:T(8,128)} %vectors.5, f32[64,128,256]{2,1,0:T(8,128)} %columns.3, f32[64,128]{1,0:T(8,128)} %diagonal.3, bf16[512,512]{1,0:T(8,128)(2,1)} %get-tuple-element.16.rows_all, f32[8,256]{1,0:T(8,128)} %get-tuple-element.17.scaling), custom_call_target="tpu_custom_call" | custom-call | flops 6442450944 | bytes 25165824 | tf_op jit(solution)/shard_map/update/pallas_call | solution.py:327
  62.4 0.0 all-to-all-done.1
  62.4 0.8 %reduce_sum.19 = f32[2,820]{1,0:T(2,128)} reduce(f32[64,2,820]{2,1,0:T(2,128)S(1)} %all-to-all-done.1, f32[]{:T(128)} %constant.69.clone.1), dimensions={0}, to_apply=%region_1.2 | reduce | flops 103320 | bytes 426404 | tf_op jit(solution)/shard_map/reduce_sum | solution.py:374
  (3 shorter events, 0.0 us)
Async XLA Ops:
  4.4 30.4 %all-to-all-start = ((f32[64,2,2176]{2,1,0:T(2,128)}), f32[64,2,2176]{2,1,0:T(2,128)S(1)}, u32[]{:S(2)}, u32[]{:S(2)}) async-start(f32[64,2,2176]{2,1,0:T(2,128)} %pick.1), calls=%async_computation | async-start | bytes 2228224 | tf_op jit(solution)/shard_map/all_to_all | solution.py:21
  16.5 15.0 %copy-start.1 = (s32[256]{0:T(256)S(1)}, s32[256]{0:T(256)}, u32[]{:S(2)}) copy-start(s32[256]{0:T(256)} %pivots.1) | copy-start | bytes 3076
  30.5 6.9 %collective-permute-start.1 = (f32[820,512]{1,0:T(8,128)}, f32[820,512]{1,0:T(8,128)S(1)}, u32[]{:S(2)}, u32[]{:S(2)}) collective-permute-start(f32[820,512]{1,0:T(8,128)} %get-tuple-element.12), channel_id=1, source_target_pairs={{0,8},{8,0},{1,9},{9,1},{2,10},{10,2},{3,11},{11,3},{4,12},{12,4},... | collective-permute-start | bytes 5038088 | tf_op jit(solution)/shard_map/ppermute | solution.py:25
  31.5 7.9 %collective-permute-start.2 = (f32[128,820]{1,0:T(8,128)}, f32[128,820]{1,0:T(8,128)S(1)}, u32[]{:S(2)}, u32[]{:S(2)}) collective-permute-start(f32[128,820]{1,0:T(8,128)} %get-tuple-element.14), channel_id=1, source_target_pairs={{0,8},{8,0},{1,9},{9,1},{2,10},{10,2},{3,11},{11,3},{4,12},{12,4},... | collective-permute-start | bytes 1259528 | tf_op jit(solution)/shard_map/ppermute | solution.py:25
  34.8 4.7 %collective-permute-start = (f32[64,2,2176]{2,1,0:T(2,128)S(1)}, f32[64,2,2176]{2,1,0:T(2,128)S(1)}, u32[]{:S(2)}, u32[]{:S(2)}) collective-permute-start(f32[64,2,2176]{2,1,0:T(2,128)S(1)} %all-to-all-done.near), channel_id=1, source_target_pairs={{0,8},{8,0},{1,9},{9,1},{2,10},{10,2},{3,11},{11,3},{4,12},{12,4},... | collective-permute-start | bytes 3342344 | tf_op jit(solution)/shard_map/ppermute | solution.py:25
  37.4 2.1 %copy-start = (f32[128,820]{1,0:T(8,128)S(1)}, f32[128,820]{1,0:T(8,128)}, u32[]{:S(2)}) copy-start(f32[128,820]{1,0:T(8,128)} %get-tuple-element.13.mine_c) | copy-start | bytes 1259524
  42.5 19.9 %all-to-all-start.1 = ((f32[64,2,820]{2,1,0:T(2,128)}), f32[64,2,820]{2,1,0:T(2,128)S(1)}, u32[]{:S(2)}, u32[]{:S(2)}) async-start(f32[64,2,820]{2,1,0:T(2,128)} %get-tuple-element.15), calls=%async_computation.1 | async-start | bytes 917504 | tf_op jit(solution)/shard_map/all_to_all | solution.py:21

commit v4 on v3

--- a/solution.py
+++ b/solution.py
@@ -224,21 +224,37 @@
     return jnp.concatenate([jnp.concatenate(vectors, axis=0), jnp.concatenate(scales, axis=0)], axis=1)
 
 
+def line_up_kernel(hot, near, out):
+    upper, lower = split(unpack(near))
+    out[...] = dot(hot[...], upper) + dot(hot[...], lower)
+
+
+def line_up(hot, near):
+    depth = (near.shape[2] - LANES) // PER_ROW
+    return pl.pallas_call(
+        line_up_kernel,
+        out_shape=jax.ShapeDtypeStruct((hot.shape[0], depth + LANES), f32),
+        in_specs=[vmem, vmem],
+        out_specs=vmem,
+        compiler_params=params(16),
+        cost_estimate=pl.CostEstimate(flops=4 * 10**8, bytes_accessed=2 * 10**6, transcendentals=0),
+        name="line_up",
+    )(hot, near)
+
+
 def choose_kernel(
-    me, near_hot, far_hot, near, far, upper_v, lower_v, mine_c, got_c, part, rows_out, scale_out, rows_all, scaling, keep_hi, keep_lo, sems
+    me, far_hot, lined, far, upper_v, lower_v, mine_c, got_c, part, rows_out, scale_out, rows_all, scaling, keep_hi, keep_lo, sems
 ):
     depth = rows_all.shape[1]
     width = depth + LANES
-    count = near_hot.shape[0]
+    count = far_hot.shape[0]
     core = (me[0] >> 3) & 1
-    near_hi, near_lo = split(unpack(near))
     far_hi, far_lo = split(unpack(far))
-    hi = dot(near_hot[...], near_hi) + dot(far_hot[...], far_hi)
-    lo = dot(near_hot[...], near_lo) + dot(far_hot[...], far_lo)
-    hi16, lo16 = hi.astype(bf16), lo.astype(bf16)
+    rows = lined[...] + (dot(far_hot[...], far_hi) + dot(far_hot[...], far_lo))
+    hi16, lo16 = split(rows)
     rows_all[:count, :] = hi16[:, :depth]
     rows_all[count:, :] = lo16[:, :depth]
-    scaling[...] = (hi[:, depth:] + lo[:, depth:]).T[:8]
+    scaling[...] = rows[:, depth:].T[:8]
     copies = [
         pltpu.make_async_copy(rows_all, rows_out, sems.at[0]),
         pltpu.make_async_copy(scaling, scale_out, sems.at[1]),
@@ -260,8 +276,8 @@
         copy.wait()
 
 
-def choose(me, near_hot, far_hot, near, far, upper_v, lower_v, mine_c, got_c):
-    count, slots = near_hot.shape
+def choose(me, far_hot, lined, far, upper_v, lower_v, mine_c, got_c):
+    count = far_hot.shape[0]
     depth = upper_v.shape[1]
     width = depth + LANES
     pairs = upper_v.shape[0]
@@ -272,7 +288,7 @@
             pltpu.HBM((2 * count, depth), bf16),
             pltpu.HBM((8, count), f32),
         ),
-        in_specs=[smem] + [vmem] * 8,
+        in_specs=[smem] + [vmem] * 7,
         out_specs=(vmem, pl.BlockSpec(memory_space=pltpu.HBM), pl.BlockSpec(memory_space=pltpu.HBM)),
         scratch_shapes=[
             pltpu.VMEM((2 * count, depth), bf16),
@@ -284,7 +300,7 @@
         compiler_params=params(24),
         cost_estimate=pl.CostEstimate(flops=2 * 10**9, bytes_accessed=6 * 10**6, transcendentals=0),
         name="choose",
-    )(me, near_hot, far_hot, near, far, upper_v, lower_v, mine_c, got_c)
+    )(me, far_hot, lined, far, upper_v, lower_v, mine_c, got_c)
 
 
 def update_kernel(vectors, columns, diagonal, rows_all, scaling, out, block, beside, sems):
@@ -368,7 +384,7 @@
 
     near, keep_c = lax.optimization_barrier((near, keep_c))
     far = sibling(near)
-    part, rows_all, scaling = choose(me, near_hot, far_hot, near, far, upper_v, lower_v, keep_c, got_c)
+    part, rows_all, scaling = choose(me, far_hot, line_up(near_hot, near), far, upper_v, lower_v, keep_c, got_c)
     arrived = exchange(part, PEERS)
     updated = update(vectors, columns, diagonal, rows_all, scaling)
     return arrived.sum(axis=0), updated

time: 63.6 us -> 64.6 us (1.016)
  starting transfers between devices: 22.9 us -> 23.7 us
    pallas_call x0 -> x1, Pallas kernels: none -> 0.81 us  [line_up(): pl.pallas_call(line_up_kernel, out_shape=jax.ShapeDtypeStruct((hot.shape[...]
    all_to_all x2, starting transfers between devices: 19.6 us -> 20.3 us  [exchange(): return lax.all_to_all(value, axes, split_axis=0, concat_axis=0, tiled=True)]
  transfers between devices with their start and end apart: 5 -> 5, of which waited for: 2 -> 1; matrix products, arithmetic and copies ran while one was open for 4% -> 4% of each run, Pallas kernels for 42% -> 42%
where the time goes in v4:
time: 64.6 us; the launch traced here: 64.2 us
  Pallas kernels  33.5 us (52%)
  starting transfers between devices  23.7 us (37%)
  other arithmetic  3.17 us (5%)
  waiting for transfers between devices  3.04 us (5%)
  between operations  0.8 us (1%)
    all_to_all x2, starting transfers between devices, exchange(): return lax.all_to_all(value, axes, split_axis=0, concat_axis=0, tiled=True)  20.3 us
    pallas_call x1, Pallas kernels, turn(): pl.pallas_call(turn_kernel, out_shape=(jax.ShapeDtypeStruct((pairs, depth...  13.9 us
    pallas_call x1, Pallas kernels, update(): pl.pallas_call(update_kernel, out_shape=jax.ShapeDtypeStruct((rows, cols)...  12.4 us
    pallas_call x1, Pallas kernels, pick(): pl.pallas_call(pick_kernel, out_shape=jax.ShapeDtypeStruct((64, SLOTS //...  3.74 us
    ppermute x3, starting transfers between devices, sibling(): return lax.ppermute(value, 'c', [(0, 1), (1, 0)])  3.4 us
    all_to_all x2, waiting for transfers between devices, exchange(): return lax.all_to_all(value, axes, split_axis=0, concat_axis=0, tiled=True)  3.03 us
    pallas_call x1, Pallas kernels, choose(): pl.pallas_call(choose_kernel, out_shape=(jax.ShapeDtypeStruct((64, count...  2.58 us
    convert_element_type x1, other arithmetic, local(): lower_v = (chip_v - upper_v).astype(bf16)  1.96 us
  transfers between devices with their start and end apart: 5, of which 1 were waited for; matrix products, arithmetic and copies ran while one was open for 4% of the time, Pallas kernels for 42%

profile of v4, /device:TPU:1, one launch (start us, length us, event | category | flops | bytes accessed | tf_op | source)
XLA Modules:
  0.0 64.2 jit_solution(2753240170958837083)
XLA Ops:
  0.6 3.7 %pick.1 = f32[64,2,2176]{2,1,0:T(2,128)} custom-call(s32[1]{0:T(128)} %bitcast.me, s32[256]{0:T(256)} %pivots.1, f32[64,128]{1,0:T(8,128)} %diagonal.3, f32[64,128,512]{2,1,0:T(8,128)} %vectors.5), custom_call_target="tpu_custom_call" | custom-call | tf_op jit(solution)/shard_map/pick/pallas_call | solution.py:102
  4.4 12.0 %all-to-all-start = ((f32[64,2,2176]{2,1,0:T(2,128)}), f32[64,2,2176]{2,1,0:T(2,128)S(1)}, u32[]{:S(2)}, u32[]{:S(2)}) async-start(f32[64,2,2176]{2,1,0:T(2,128)} %pick.1), calls=%async_computation | async-start | bytes 2228224 | tf_op jit(solution)/shard_map/all_to_all | solution.py:21
  16.4 0.0 copy-start.2
  16.4 13.9 %turn.1 = (f32[820,512]{1,0:T(8,128)}, f32[128,820]{1,0:T(8,128)}, f32[128,820]{1,0:T(8,128)}) custom-call(s32[1]{0:T(128)} %bitcast.me, f32[40,1024]{1,0:T(8,128)} %bitcast.2, f32[64,128,512]{2,1,0:T(8,128)} %vectors.5, f32[64,128,256]{2,1,0:T(8,128)} %columns.3), custom_call_target="tpu_custom_call" | custom-call | flops 10000000000 | bytes 25165824 | tf_op jit(solution)/shard_map/turn/pallas_call | solution.py:189
  30.4 0.0 copy-start.1
  30.4 1.0 %collective-permute-start.1 = (f32[820,512]{1,0:T(8,128)}, f32[820,512]{1,0:T(8,128)}, u32[]{:S(2)}, u32[]{:S(2)}) collective-permute-start(f32[820,512]{1,0:T(8,128)} %get-tuple-element.12), channel_id=1, source_target_pairs={{0,8},{8,0},{1,9},{9,1},{2,10},{10,2},{3,11},{11,3},{4,12},{12,4},... | collective-permute-start | bytes 5038088 | tf_op jit(solution)/shard_map/ppermute | solution.py:25
  31.4 0.1 collective-permute-start.2
  31.5 0.0 copy-done.2
  31.5 0.2 convert_reduce_fusion
  31.7 3.0 %all-to-all-done.near = f32[64,2,2176]{2,1,0:T(2,128)S(1)} async-done(((f32[64,2,2176]{2,1,0:T(2,128)}), f32[64,2,2176]{2,1,0:T(2,128)S(1)}, u32[]{:S(2)}, u32[]{:S(2)}) %all-to-all-start) | async-done | bytes 1114144 | tf_op jit(solution)/shard_map/all_to_all | solution.py:21
  34.7 2.3 %collective-permute-start = (f32[64,2,2176]{2,1,0:T(2,128)S(1)}, f32[64,2,2176]{2,1,0:T(2,128)S(1)}, u32[]{:S(2)}, u32[]{:S(2)}) collective-permute-start(f32[64,2,2176]{2,1,0:T(2,128)S(1)} %all-to-all-done.near), channel_id=1, source_target_pairs={{0,8},{8,0},{1,9},{9,1},{2,10},{10,2},{3,11},{11,3},{4,12},{12,4},... | collective-permute-start | bytes 3342344 | tf_op jit(solution)/shard_map/ppermute | solution.py:25
  37.0 0.1 fusion.2.hot
  37.1 0.1 fusion.1.far_hot
  37.3 0.8 %line_up.1.lined = f32[256,640]{1,0:T(8,128)S(1)} custom-call(bf16[256,512]{1,0:T(8,128)(2,1)S(1)} %fusion.2.hot, f32[64,2,2176]{2,1,0:T(2,128)S(1)} %all-to-all-done.near), custom_call_target="tpu_custom_call" | custom-call | flops 400000000 | bytes 2000000 | tf_op jit(solution)/shard_map/line_up/pallas_call | solution.py:234
  38.1 0.0 copy-start
  38.1 0.0 collective-permute-done.1
  38.1 0.0 copy-done.1
  38.1 2.0 %fusion = (bf16[820,512]{1,0:T(8,128)(2,1)S(1)}, bf16[820,512]{1,0:T(8,128)(2,1)S(1)}) fusion(f32[820,512]{1,0:T(8,128)S(1)} %copy-done.1, f32[820,512]{1,0:T(8,128)} %collective-permute-done.1), kind=kLoop, calls=%fused_computation.2 | loop fusion | flops 2099200 | bytes 5038080 | tf_op jit(solution)/shard_map/convert_element_type | solution.py:382
  40.1 0.0 collective-permute-done.2.got_c
  40.1 0.0 collective-permute-done.far
  40.1 0.0 copy-done
  40.1 2.6 %choose.1 = (f32[64,2,820]{2,1,0:T(2,128)}, bf16[512,512]{1,0:T(8,128)(2,1)}, f32[8,256]{1,0:T(8,128)}) custom-call(s32[1]{0:T(128)} %bitcast.me, bf16[256,512]{1,0:T(8,128)(2,1)S(1)} %fusion.1.far_hot, f32[256,640]{1,0:T(8,128)S(1)} %line_up.1.lined, f32[64,2,2176]{2,1,0:T(2,128)S(1)} %collective-permute-done.far, ...), custom_call_target="tpu_custom_call" | custom-call | flops 2000000000 | bytes 6000000 | tf_op jit(solution)/shard_map/choose/pallas_call | solution.py:284
  42.7 8.3 %all-to-all-start.1 = ((f32[64,2,820]{2,1,0:T(2,128)}), f32[64,2,820]{2,1,0:T(2,128)S(1)}, u32[]{:S(2)}, u32[]{:S(2)}) async-start(f32[64,2,820]{2,1,0:T(2,128)} %get-tuple-element.15), calls=%async_computation.1 | async-start | bytes 917504 | tf_op jit(solution)/shard_map/all_to_all | solution.py:21
  51.0 12.4 %update.1 = f32[64,128]{1,0:T(8,128)} custom-call(f32[64,128,512]{2,1,0:T(8,128)} %vectors.5, f32[64,128,256]{2,1,0:T(8,128)} %columns.3, f32[64,128]{1,0:T(8,128)} %diagonal.3, bf16[512,512]{1,0:T(8,128)(2,1)} %get-tuple-element.16.rows_all, f32[8,256]{1,0:T(8,128)} %get-tuple-element.17.scaling), custom_call_target="tpu_custom_call" | custom-call | flops 6442450944 | bytes 25165824 | tf_op jit(solution)/shard_map/update/pallas_call | solution.py:343
  63.4 0.0 all-to-all-done.1
  63.4 0.8 %reduce_sum.19 = f32[2,820]{1,0:T(2,128)} reduce(f32[64,2,820]{2,1,0:T(2,128)S(1)} %all-to-all-done.1, f32[]{:T(128)} %constant.69.clone.1), dimensions={0}, to_apply=%region_1.2 | reduce | flops 103320 | bytes 426404 | tf_op jit(solution)/shard_map/reduce_sum | solution.py:390
  (3 shorter events, 0.0 us)
Async XLA Ops:
  4.4 30.3 %all-to-all-start = ((f32[64,2,2176]{2,1,0:T(2,128)}), f32[64,2,2176]{2,1,0:T(2,128)S(1)}, u32[]{:S(2)}, u32[]{:S(2)}) async-start(f32[64,2,2176]{2,1,0:T(2,128)} %pick.1), calls=%async_computation | async-start | bytes 2228224 | tf_op jit(solution)/shard_map/all_to_all | solution.py:21
  16.4 15.1 %copy-start.2 = (s32[256]{0:T(256)S(1)}, s32[256]{0:T(256)}, u32[]{:S(2)}) copy-start(s32[256]{0:T(256)} %pivots.1) | copy-start | bytes 3076
  30.4 7.7 %copy-start.1 = (f32[820,512]{1,0:T(8,128)S(1)}, f32[820,512]{1,0:T(8,128)}, u32[]{:S(2)}) copy-start(f32[820,512]{1,0:T(8,128)} %get-tuple-element.12) | copy-start | bytes 5038084
  30.4 7.7 %collective-permute-start.1 = (f32[820,512]{1,0:T(8,128)}, f32[820,512]{1,0:T(8,128)}, u32[]{:S(2)}, u32[]{:S(2)}) collective-permute-start(f32[820,512]{1,0:T(8,128)} %get-tuple-element.12), channel_id=1, source_target_pairs={{0,8},{8,0},{1,9},{9,1},{2,10},{10,2},{3,11},{11,3},{4,12},{12,4},... | collective-permute-start | bytes 5038088 | tf_op jit(solution)/shard_map/ppermute | solution.py:25
  31.4 8.7 %collective-permute-start.2 = (f32[128,820]{1,0:T(8,128)}, f32[128,820]{1,0:T(8,128)S(1)}, u32[]{:S(2)}, u32[]{:S(2)}) collective-permute-start(f32[128,820]{1,0:T(8,128)} %get-tuple-element.14), channel_id=1, source_target_pairs={{0,8},{8,0},{1,9},{9,1},{2,10},{10,2},{3,11},{11,3},{4,12},{12,4},... | collective-permute-start | bytes 1259528 | tf_op jit(solution)/shard_map/ppermute | solution.py:25
  34.7 5.4 %collective-permute-start = (f32[64,2,2176]{2,1,0:T(2,128)S(1)}, f32[64,2,2176]{2,1,0:T(2,128)S(1)}, u32[]{:S(2)}, u32[]{:S(2)}) collective-permute-start(f32[64,2,2176]{2,1,0:T(2,128)S(1)} %all-to-all-done.near), channel_id=1, source_target_pairs={{0,8},{8,0},{1,9},{9,1},{2,10},{10,2},{3,11},{11,3},{4,12},{12,4},... | collective-permute-start | bytes 3342344 | tf_op jit(solution)/shard_map/ppermute | solution.py:25
  38.1 2.0 %copy-start = (f32[128,820]{1,0:T(8,128)S(1)}, f32[128,820]{1,0:T(8,128)}, u32[]{:S(2)}) copy-start(f32[128,820]{1,0:T(8,128)} %get-tuple-element.13.mine_c) | copy-start | bytes 1259524
  42.7 20.7 %all-to-all-start.1 = ((f32[64,2,820]{2,1,0:T(2,128)}), f32[64,2,820]{2,1,0:T(2,128)S(1)}, u32[]{:S(2)}, u32[]{:S(2)}) async-start(f32[64,2,820]{2,1,0:T(2,128)} %get-tuple-element.15), calls=%async_computation.1 | async-start | bytes 917504 | tf_op jit(solution)/shard_map/all_to_all | solution.py:21

commit v5 on v3

--- a/solution.py
+++ b/solution.py
@@ -366,7 +366,7 @@
     lower_v = (chip_v - upper_v).astype(bf16)
     upper_v = upper_v.astype(bf16)
 
-    near, keep_c = lax.optimization_barrier((near, keep_c))
+    near, keep_c, near_hot, far_hot = lax.optimization_barrier((near, keep_c, near_hot, far_hot))
     far = sibling(near)
     part, rows_all, scaling = choose(me, near_hot, far_hot, near, far, upper_v, lower_v, keep_c, got_c)
     arrived = exchange(part, PEERS)

time: 63.6 us -> 63.6 us (level)
    ppermute x3, waiting for transfers between devices: 0.13 us -> 1.14 us  [sibling(): return lax.ppermute(value, 'c', [(0, 1), (1, 0)])]
    all_to_all x2, starting transfers between devices: 19.6 us -> 18.8 us  [exchange(): return lax.all_to_all(value, axes, split_axis=0, concat_axis=0, tiled=True)]
where the time goes in v5:
time: 63.6 us; the launch traced here: 63.2 us
  Pallas kernels  33.2 us (52%)
  starting transfers between devices  22.5 us (35%)
  waiting for transfers between devices  3.74 us (6%)
  other arithmetic  3.11 us (5%)
  between operations  0.74 us (1%)
    all_to_all x2, starting transfers between devices, exchange(): return lax.all_to_all(value, axes, split_axis=0, concat_axis=0, tiled=True)  18.8 us
    pallas_call x1, Pallas kernels, turn(): pl.pallas_call(turn_kernel, out_shape=(jax.ShapeDtypeStruct((pairs, depth...  13.9 us
    pallas_call x1, Pallas kernels, update(): pl.pallas_call(update_kernel, out_shape=jax.ShapeDtypeStruct((rows, cols)...  12.4 us
    pallas_call x1, Pallas kernels, pick(): pl.pallas_call(pick_kernel, out_shape=jax.ShapeDtypeStruct((64, SLOTS //...  3.82 us
    ppermute x3, starting transfers between devices, sibling(): return lax.ppermute(value, 'c', [(0, 1), (1, 0)])  3.64 us
    pallas_call x1, Pallas kernels, choose(): pl.pallas_call(choose_kernel, out_shape=(jax.ShapeDtypeStruct((64, count...  2.99 us
    all_to_all x2, waiting for transfers between devices, exchange(): return lax.all_to_all(value, axes, split_axis=0, concat_axis=0, tiled=True)  2.59 us
    convert_element_type x1, other arithmetic, local(): lower_v = (chip_v - upper_v).astype(bf16)  1.96 us
  transfers between devices with their start and end apart: 5, of which 2 were waited for; matrix products, arithmetic and copies ran while one was open for 4% of the time, Pallas kernels for 42%

profile of v5, /device:TPU:1, one launch (start us, length us, event | category | flops | bytes accessed | tf_op | source)
XLA Modules:
  0.0 63.2 jit_solution(7459598061051219003)
XLA Ops:
  0.6 3.8 %pick.1 = f32[64,2,2176]{2,1,0:T(2,128)} custom-call(s32[1]{0:T(128)} %bitcast.me, s32[256]{0:T(256)} %pivots.1, f32[64,128]{1,0:T(8,128)} %diagonal.3, f32[64,128,512]{2,1,0:T(8,128)} %vectors.5), custom_call_target="tpu_custom_call" | custom-call | tf_op jit(solution)/shard_map/pick/pallas_call | solution.py:102
  4.5 11.9 %all-to-all-start = ((f32[64,2,2176]{2,1,0:T(2,128)}), f32[64,2,2176]{2,1,0:T(2,128)S(1)}, u32[]{:S(2)}, u32[]{:S(2)}) async-start(f32[64,2,2176]{2,1,0:T(2,128)} %pick.1), calls=%async_computation | async-start | bytes 2228224 | tf_op jit(solution)/shard_map/all_to_all | solution.py:21
  16.4 0.0 copy-start.1
  16.4 13.9 %turn.1 = (f32[820,512]{1,0:T(8,128)}, f32[128,820]{1,0:T(8,128)}, f32[128,820]{1,0:T(8,128)}) custom-call(s32[1]{0:T(128)} %bitcast.me, f32[40,1024]{1,0:T(8,128)} %bitcast.2, f32[64,128,512]{2,1,0:T(8,128)} %vectors.5, f32[64,128,256]{2,1,0:T(8,128)} %columns.3), custom_call_target="tpu_custom_call" | custom-call | flops 10000000000 | bytes 25165824 | tf_op jit(solution)/shard_map/turn/pallas_call | solution.py:189
  30.4 1.1 %collective-permute-start.1 = (f32[820,512]{1,0:T(8,128)}, f32[820,512]{1,0:T(8,128)S(1)}, u32[]{:S(2)}, u32[]{:S(2)}) collective-permute-start(f32[820,512]{1,0:T(8,128)} %get-tuple-element.16), channel_id=1, source_target_pairs={{0,8},{8,0},{1,9},{9,1},{2,10},{10,2},{3,11},{11,3},{4,12},{12,4},... | collective-permute-start | bytes 5038088 | tf_op jit(solution)/shard_map/ppermute | solution.py:25
  31.5 0.0 copy-done.1
  31.5 0.2 convert_reduce_fusion
  31.7 0.2 fusion.1
  31.9 2.6 %all-to-all-done.near = f32[64,2,2176]{2,1,0:T(2,128)S(1)} async-done(((f32[64,2,2176]{2,1,0:T(2,128)}), f32[64,2,2176]{2,1,0:T(2,128)S(1)}, u32[]{:S(2)}, u32[]{:S(2)}) %all-to-all-start) | async-done | bytes 1114144 | tf_op jit(solution)/shard_map/all_to_all | solution.py:21
  34.5 2.5 %collective-permute-start = (f32[64,2,2176]{2,1,0:T(2,128)S(1)}, f32[64,2,2176]{2,1,0:T(2,128)S(1)}, u32[]{:S(2)}, u32[]{:S(2)}) collective-permute-start(f32[64,2,2176]{2,1,0:T(2,128)S(1)} %all-to-all-done.near), channel_id=1, source_target_pairs={{0,8},{8,0},{1,9},{9,1},{2,10},{10,2},{3,11},{11,3},{4,12},{12,4},... | collective-permute-start | bytes 3342344 | tf_op jit(solution)/shard_map/ppermute | solution.py:25
  37.0 0.0 copy-start
  37.0 0.0 collective-permute-start.2
  37.0 0.0 collective-permute-done.1
  37.0 2.0 %fusion = (bf16[820,512]{1,0:T(8,128)(2,1)S(1)}, bf16[820,512]{1,0:T(8,128)(2,1)S(1)}) fusion(f32[820,512]{1,0:T(8,128)} %get-tuple-element.16, f32[820,512]{1,0:T(8,128)S(1)} %collective-permute-done.1), kind=kLoop, calls=%fused_computation.2 | loop fusion | flops 2099200 | bytes 5038080 | tf_op jit(solution)/shard_map/convert_element_type | solution.py:366
  39.0 1.1 %collective-permute-done.2.got_c = f32[128,820]{1,0:T(8,128)S(1)} collective-permute-done((f32[128,820]{1,0:T(8,128)}, f32[128,820]{1,0:T(8,128)S(1)}, u32[]{:S(2)}, u32[]{:S(2)}) %collective-permute-start.2) | collective-permute-done | bytes 419872 | tf_op jit(solution)/shard_map/ppermute | solution.py:25
  40.1 0.0 collective-permute-done.far
  40.1 0.0 copy-done
  40.1 3.0 %choose.1 = (f32[64,2,820]{2,1,0:T(2,128)}, bf16[512,512]{1,0:T(8,128)(2,1)}, f32[8,256]{1,0:T(8,128)}) custom-call(s32[1]{0:T(128)} %bitcast.me, bf16[256,512]{1,0:T(8,128)(2,1)S(1)} %get-tuple-element.13.near_hot, bf16[256,512]{1,0:T(8,128)(2,1)S(1)} %get-tuple-element.14.far_hot, f32[64,2,2176]{2,1,0:T(2,128)S(1)} %all-to-all-done.near, ...), custom_call_target="tpu_custom_call" | custom-call | flops 2000000000 | bytes 6000000 | tf_op jit(solution)/shard_map/choose/pallas_call | solution.py:268
  43.1 6.9 %all-to-all-start.1 = ((f32[64,2,820]{2,1,0:T(2,128)}), f32[64,2,820]{2,1,0:T(2,128)S(1)}, u32[]{:S(2)}, u32[]{:S(2)}) async-start(f32[64,2,820]{2,1,0:T(2,128)} %get-tuple-element.19), calls=%async_computation.1 | async-start | bytes 917504 | tf_op jit(solution)/shard_map/all_to_all | solution.py:21
  50.0 12.4 %update.1 = f32[64,128]{1,0:T(8,128)} custom-call(f32[64,128,512]{2,1,0:T(8,128)} %vectors.5, f32[64,128,256]{2,1,0:T(8,128)} %columns.3, f32[64,128]{1,0:T(8,128)} %diagonal.3, bf16[512,512]{1,0:T(8,128)(2,1)} %get-tuple-element.20.rows_all, f32[8,256]{1,0:T(8,128)} %get-tuple-element.21.scaling), custom_call_target="tpu_custom_call" | custom-call | flops 6442450944 | bytes 25165824 | tf_op jit(solution)/shard_map/update/pallas_call | solution.py:327
  62.4 0.0 all-to-all-done.1
  62.4 0.8 %reduce_sum.19 = f32[2,820]{1,0:T(2,128)} reduce(f32[64,2,820]{2,1,0:T(2,128)S(1)} %all-to-all-done.1, f32[]{:T(128)} %constant.69.clone.1), dimensions={0}, to_apply=%region_1.2 | reduce | flops 103320 | bytes 426404 | tf_op jit(solution)/shard_map/reduce_sum | solution.py:374
  (3 shorter events, 0.0 us)
Async XLA Ops:
  4.5 30.0 %all-to-all-start = ((f32[64,2,2176]{2,1,0:T(2,128)}), f32[64,2,2176]{2,1,0:T(2,128)S(1)}, u32[]{:S(2)}, u32[]{:S(2)}) async-start(f32[64,2,2176]{2,1,0:T(2,128)} %pick.1), calls=%async_computation | async-start | bytes 2228224 | tf_op jit(solution)/shard_map/all_to_all | solution.py:21
  16.4 15.1 %copy-start.1 = (s32[256]{0:T(256)S(1)}, s32[256]{0:T(256)}, u32[]{:S(2)}) copy-start(s32[256]{0:T(256)} %pivots.1) | copy-start | bytes 3076
  30.4 6.6 %collective-permute-start.1 = (f32[820,512]{1,0:T(8,128)}, f32[820,512]{1,0:T(8,128)S(1)}, u32[]{:S(2)}, u32[]{:S(2)}) collective-permute-start(f32[820,512]{1,0:T(8,128)} %get-tuple-element.16), channel_id=1, source_target_pairs={{0,8},{8,0},{1,9},{9,1},{2,10},{10,2},{3,11},{11,3},{4,12},{12,4},... | collective-permute-start | bytes 5038088 | tf_op jit(solution)/shard_map/ppermute | solution.py:25
  34.5 5.6 %collective-permute-start = (f32[64,2,2176]{2,1,0:T(2,128)S(1)}, f32[64,2,2176]{2,1,0:T(2,128)S(1)}, u32[]{:S(2)}, u32[]{:S(2)}) collective-permute-start(f32[64,2,2176]{2,1,0:T(2,128)S(1)} %all-to-all-done.near), channel_id=1, source_target_pairs={{0,8},{8,0},{1,9},{9,1},{2,10},{10,2},{3,11},{11,3},{4,12},{12,4},... | collective-permute-start | bytes 3342344 | tf_op jit(solution)/shard_map/ppermute | solution.py:25
  37.0 3.1 %copy-start = (f32[128,820]{1,0:T(8,128)S(1)}, f32[128,820]{1,0:T(8,128)}, u32[]{:S(2)}) copy-start(f32[128,820]{1,0:T(8,128)} %get-tuple-element.17.mine_c) | copy-start | bytes 1259524
  37.0 3.1 %collective-permute-start.2 = (f32[128,820]{1,0:T(8,128)}, f32[128,820]{1,0:T(8,128)S(1)}, u32[]{:S(2)}, u32[]{:S(2)}) collective-permute-start(f32[128,820]{1,0:T(8,128)} %get-tuple-element.18), channel_id=1, source_target_pairs={{0,8},{8,0},{1,9},{9,1},{2,10},{10,2},{3,11},{11,3},{4,12},{12,4},... | collective-permute-start | bytes 1259528 | tf_op jit(solution)/shard_map/ppermute | solution.py:25
  43.1 19.3 %all-to-all-start.1 = ((f32[64,2,820]{2,1,0:T(2,128)}), f32[64,2,820]{2,1,0:T(2,128)S(1)}, u32[]{:S(2)}, u32[]{:S(2)}) async-start(f32[64,2,820]{2,1,0:T(2,128)} %get-tuple-element.19), calls=%async_computation.1 | async-start | bytes 917504 | tf_op jit(solution)/shard_map/all_to_all | solution.py:21
